TPU v7x, 256 devices: a whole 4x4x8 slice. The times are simulated.
256 devices in a mesh: section: 4 (over x_lo, core), dp: 64 (over z, x_hi, y).
Axes of the slice: x: 4 (x_hi: 2, x_lo: 2; x = x_hi * 2 + x_lo), y: 4, z: 8, core: 2. Of those that a mesh axis runs over, the one named last changes fastest.
Arguments:
- obs_features: bfloat16 [4, 2048, 1024], P(None, 'dp'), may hold values from -1.1953125 to 1.1953125
- w_input: bfloat16 [4, 1024, 4096], P('section'), may hold values from -1 to 1
- w_recurrent: bfloat16 [4, 1024, 4096], P('section', None, 'dp'), may hold values from -0.1875 to 0.1875
- bias: float32 [4, 4096], P('section'), may hold values from -3 to 3
- stored_states: bfloat16 [4, 4, 2048, 2048], P('section', None, 'dp'), may hold values from -3 to 3
- state_owner: int32 [2048], P('dp'), may hold values from 0 to 3
- burn_steps: int32 [2048], P('dp'), may hold values from 1 to 2
- valid_steps: int32 [2048], P('dp'), may hold values from 3 to 4
- cotangent: bfloat16 [4, 2048, 1024], P(None, 'dp'), may hold values from -3 to 3
Outputs:
- hidden_all: bfloat16 [4, 4, 2048, 1024], P('section', None, 'dp')
- grad_recurrent: float32 [4, 1024, 4096], P('section', None, 'dp')
- grad_bias: float32 [4, 4096], P('section', 'dp')
All inputs are finite; a program needn't handle non-finite values.
Results may differ from a plain program's by a relative error of at most 0.017.
Values may be sent and summed in bfloat16 or wider, within the bound.
A program may use at most 128 MiB of HBM per device.

v0:
```python
from functools import partial

import jax
import jax.numpy as jnp
from jax import lax
from jax.sharding import Mesh
from jax.sharding import PartitionSpec as P

SPAN = 2
SECTION = ("section_0", "section_1")


def split_up(array, dim, peers):
    lengths = array.shape
    parts = array.reshape(*lengths[:dim], peers, lengths[dim] // peers, *lengths[dim + 1 :])
    return jnp.moveaxis(parts, dim, 0)


def scatter_pairs(array, chips, core, dim):
    sizes = (lax.axis_size(chips), lax.axis_size(core))
    parts = split_up(array, dim, sizes[0] * sizes[1])
    inside = parts.shape[1:]
    parts = parts.reshape(*sizes, *inside).swapaxes(0, 1).reshape(-1, *inside)
    parts = lax.psum_scatter(parts, core, scatter_dimension=0, tiled=True)
    return lax.psum_scatter(parts, chips, scatter_dimension=0, tiled=True)[0]


def from_behind(array, axis, by):
    peers = lax.axis_size(axis)
    pairs = [(i, i + by) for i in range(peers) if 0 <= i + by < peers]
    return lax.ppermute(array, axis, pairs)


def lstm_cell(preact, cell_prev):
    breadth = cell_prev.shape[-1]
    in_gate = jax.nn.sigmoid(preact[:, :breadth])
    forget = jax.nn.sigmoid(preact[:, breadth : 2 * breadth])
    candidate = jnp.tanh(preact[:, 2 * breadth : 3 * breadth])
    out_gate = jax.nn.sigmoid(preact[:, 3 * breadth :])
    cell_new = forget * cell_prev + in_gate * candidate
    hidden_new = (out_gate * jnp.tanh(cell_new)).astype(jnp.bfloat16)
    gate_vals = jnp.concatenate([in_gate, forget, candidate, out_gate], axis=-1)
    return (hidden_new, cell_new, gate_vals)


def forward_span(inputs, w_in, w_rec, bias_row, hidden_start, cell_start):
    step_count, seq_rows, breadth = inputs.shape
    projected = jnp.dot(
        inputs.reshape(step_count * seq_rows, breadth), w_in, preferred_element_type=jnp.float32
    )
    projected = projected.reshape(step_count, seq_rows, -1) + bias_row

    def advance(carried, proj_row):
        hidden_prev, cell_prev = carried
        preact = proj_row + jnp.dot(hidden_prev, w_rec, preferred_element_type=jnp.float32)
        hidden_new, cell_new, gate_vals = lstm_cell(preact, cell_prev)
        return ((hidden_new, cell_new), (hidden_new, cell_new, gate_vals))

    (hidden_end, cell_end), (hidden_seq, cell_seq, gate_seq) = lax.scan(
        advance, (hidden_start, cell_start), projected
    )
    return (hidden_seq, cell_seq, gate_seq, hidden_end, cell_end)


def times_transposed(operand, matrix):
    return lax.dot_general(
        operand, matrix, (((1,), (1,)), ((), ())), preferred_element_type=jnp.float32
    )


def backward_span(above_grads, cell_now, cell_old, gate_seq, live_mask, w_rec, grad_h, grad_c):

    def retreat(carried, inputs):
        grad_hidden, grad_cell = carried
        grad_out, cell_cur, cell_before, gate_vals, alive_row = inputs
        breadth = cell_cur.shape[-1]
        in_gate = gate_vals[:, :breadth]
        forget = gate_vals[:, breadth : 2 * breadth]
        candidate = gate_vals[:, 2 * breadth : 3 * breadth]
        out_gate = gate_vals[:, 3 * breadth :]
        total_h = grad_out.astype(jnp.float32) + grad_hidden
        squashed = jnp.tanh(cell_cur)
        total_c = grad_cell + total_h * out_gate * (1.0 - squashed * squashed)
        grad_pre = (
            jnp.concatenate(
                [
                    total_c * candidate * in_gate * (1.0 - in_gate),
                    total_c * cell_before * forget * (1.0 - forget),
                    total_c * in_gate * (1.0 - candidate * candidate),
                    total_h * squashed * out_gate * (1.0 - out_gate),
                ],
                axis=-1,
            )
            * alive_row[:, None]
        )
        gate_grads = grad_pre.astype(jnp.bfloat16)
        return (
            (times_transposed(gate_grads, w_rec), total_c * forget * alive_row[:, None]),
            gate_grads,
        )

    (grad_h_end, grad_c_end), gate_grads = lax.scan(
        retreat,
        (grad_h, grad_c),
        (above_grads, cell_now, cell_old, gate_seq, live_mask),
        reverse=True,
    )
    return (gate_grads, grad_h_end, grad_c_end)


def on_device(
    obs_features,
    w_input,
    w_recurrent,
    bias,
    stored_states,
    state_owner,
    burn_steps,
    valid_steps,
    cotangent,
):
    section_index = lax.axis_index(SECTION)
    sections = lax.axis_size(SECTION)
    step_count, seq_rows, breadth = obs_features.shape
    gate_width = 4 * breadth
    w_in = w_input[0]
    bias_row = bias[0]
    owned_rows = (state_owner == section_index)[None, :, None]
    state_table = jnp.where(owned_rows, stored_states[0].astype(jnp.float32), jnp.float32(0.0))
    delivered = scatter_pairs(state_table.astype(jnp.bfloat16), "section_0", "section_1", 0).astype(
        jnp.float32
    )[0]
    hidden_start = delivered[:, :breadth].astype(jnp.bfloat16)
    cell_start = delivered[:, breadth:]
    w_rec = lax.all_gather(w_recurrent[0], "dp", axis=1, tiled=True)
    positions = jnp.arange(step_count, dtype=jnp.int32)[:, None]
    live_mask = ((positions >= burn_steps[None, :]) & (positions < valid_steps[None, :])).astype(
        jnp.float32
    )
    block_total = step_count // SPAN
    block_len = step_count // block_total
    tick_count = block_total + sections - 1

    def advance_block(inputs, offset, carried):
        hidden_now, cell_now, hidden_buf, cell_buf, gate_buf = carried
        hidden_seq, cell_seq, gate_seq, hidden_end, cell_end = forward_span(
            inputs, w_in, w_rec, bias_row, hidden_now, cell_now
        )
        hidden_buf = lax.dynamic_update_slice_in_dim(hidden_buf, hidden_seq, offset, 0)
        cell_buf = lax.dynamic_update_slice_in_dim(cell_buf, cell_seq, offset, 0)
        gate_buf = lax.dynamic_update_slice_in_dim(gate_buf, gate_seq, offset, 0)
        return ((hidden_end, cell_end, hidden_buf, cell_buf, gate_buf), hidden_seq)

    def keep_block(carried):
        return (carried, jnp.zeros((block_len, seq_rows, breadth), jnp.bfloat16))

    carried = (
        hidden_start,
        cell_start,
        jnp.zeros((step_count, seq_rows, breadth), jnp.bfloat16),
        jnp.zeros((step_count, seq_rows, breadth), jnp.float32),
        jnp.zeros((step_count, seq_rows, gate_width), jnp.float32),
    )
    incoming = jnp.zeros((block_len, seq_rows, breadth), jnp.bfloat16)
    for tick_index in range(tick_count):
        block_index = tick_index - section_index
        active = (block_index >= 0) & (block_index < block_total)
        offset = jnp.clip(block_index, 0, block_total - 1) * block_len
        first_block = lax.dynamic_slice_in_dim(obs_features, offset, block_len, 0)
        inputs = jnp.where(section_index == 0, first_block, incoming)
        carried, outgoing = lax.cond(
            active, partial(advance_block, inputs, offset), keep_block, carried
        )
        if tick_index + 1 < tick_count:
            incoming = from_behind(outgoing, SECTION, 1)
    hidden_buf = carried[2]
    cell_buf = carried[3]
    gate_buf = carried[4]
    cell_full = jnp.concatenate([cell_start[None], cell_buf], axis=0)

    def retreat_block(above_grads, offset, back_state):
        grad_h, grad_c, grad_buf = back_state
        cell_cur = lax.dynamic_slice_in_dim(cell_buf, offset, block_len, 0)
        cell_before = lax.dynamic_slice_in_dim(cell_full, offset, block_len, 0)
        gate_vals = lax.dynamic_slice_in_dim(gate_buf, offset, block_len, 0)
        alive_rows = lax.dynamic_slice_in_dim(live_mask, offset, block_len, 0)
        gate_grads, grad_h, grad_c = backward_span(
            above_grads, cell_cur, cell_before, gate_vals, alive_rows, w_rec, grad_h, grad_c
        )
        grad_buf = lax.dynamic_update_slice_in_dim(grad_buf, gate_grads, offset, 0)

        def lower_input(values):
            return (
                times_transposed(values.reshape(-1, gate_width), w_in)
                .reshape(block_len, seq_rows, breadth)
                .astype(jnp.bfloat16)
            )

        def no_input(values):
            return jnp.zeros((block_len, seq_rows, breadth), jnp.bfloat16)

        lower_grads = lax.cond(section_index > 0, lower_input, no_input, gate_grads)
        return ((grad_h, grad_c, grad_buf), lower_grads)

    def keep_back(back_state):
        return (back_state, jnp.zeros((block_len, seq_rows, breadth), jnp.bfloat16))

    back_state = (
        jnp.zeros((seq_rows, breadth), jnp.float32),
        jnp.zeros((seq_rows, breadth), jnp.float32),
        jnp.zeros((step_count, seq_rows, gate_width), jnp.bfloat16),
    )
    arriving = jnp.zeros((block_len, seq_rows, breadth), jnp.bfloat16)
    for tick_index in range(tick_count):
        block_index = block_total - 1 - (tick_index - (sections - 1 - section_index))
        active = (block_index >= 0) & (block_index < block_total)
        offset = jnp.clip(block_index, 0, block_total - 1) * block_len
        top_block = lax.dynamic_slice_in_dim(cotangent, offset, block_len, 0)
        above_grads = jnp.where(section_index == sections - 1, top_block, arriving)
        back_state, sending = lax.cond(
            active, partial(retreat_block, above_grads, offset), keep_back, back_state
        )
        if tick_index + 1 < tick_count:
            arriving = from_behind(sending, SECTION, -1)
    gate_rows = back_state[2].reshape(step_count * seq_rows, gate_width)
    prev_rows = jnp.concatenate([hidden_start[None], hidden_buf[:-1]], axis=0).reshape(
        step_count * seq_rows, breadth
    )
    grad_cols = lax.all_to_all(gate_rows, "dp", split_axis=1, concat_axis=0, tiled=True)
    weight_grad = lax.dot_general(
        lax.all_gather(prev_rows, "dp", axis=0, tiled=True),
        grad_cols,
        (((0,), (0,)), ((), ())),
        preferred_element_type=jnp.float32,
    )
    bias_grad = jnp.sum(grad_cols, axis=0, dtype=jnp.float32)
    return (hidden_buf[None], weight_grad[None], bias_grad[None])


def solution(mesh):
    split = Mesh(mesh.devices.reshape(2, 2, mesh.shape["dp"]), ("section_0", "section_1", "dp"))
    return jax.shard_map(
        on_device,
        mesh=split,
        in_specs=(
            P(None, "dp", None),
            P(SECTION, None, None),
            P(SECTION, None, "dp"),
            P(SECTION, None),
            P(SECTION, None, "dp", None),
            P("dp"),
            P("dp"),
            P("dp"),
            P(None, "dp", None),
        ),
        out_specs=(P(SECTION, None, "dp", None), P(SECTION, None, "dp"), P(SECTION, "dp")),
        check_vma=False,
    )
```

profile of v0, /device:TPU:24, one launch (start us, length us, event | category | flops | bytes accessed | tf_op | source)
XLA Modules:
  0.0 632.9 jit_solution(7293564642440216710)
XLA Ops:
  8.7 2.0 fusion.192
  10.8 16.5 %reduce-scatter.3.cloned.1.call-done = bf16[2,1,32,2048]{3,2,1,0:T(8,128)(2,1)} async-done(((bf16[4,1,32,2048]{3,2,1,0:T(8,128)(2,1)}), bf16[2,1,32,2048]{3,2,1,0:T(8,128)(2,1)}) %reduce-scatter.3.cloned.1.call-update) | async-done | bytes 262160 | tf_op jit(solution)/shard_map/reduce_scatter | solution.py:24
  28.0 20.0 %reduce-scatter.5.cloned.1.call-done = bf16[1,1,32,2048]{3,2,1,0:T(8,128)(2,1)} async-done(((bf16[2,1,32,2048]{3,2,1,0:T(8,128)(2,1)}), bf16[1,1,32,2048]{3,2,1,0:T(8,128)(2,1)}) %reduce-scatter.5.cloned.1.call-update) | async-done | bytes 131088 | tf_op jit(solution)/shard_map/reduce_scatter | solution.py:25
  48.0 1.6 fusion.193
  49.6 133.9 %all-gather.6.cloned.1.call-done = bf16[1,1024,4096]{1,2,0:T(8,128)(2,1)} async-done(((bf16[1,1024,64]{1,2,0:T(8,128)(2,1)}), bf16[1,1024,4096]{1,2,0:T(8,128)(2,1)}) %all-gather.6.cloned.1.call-update) | async-done | bytes 8388624 | tf_op jit(solution)/shard_map/all_gather | solution.py:135
  183.5 34.6 %conditional.14 = (bf16[32,1024]{1,0:T(8,128)(2,1)S(1)}, f32[32,1024]{1,0:T(8,128)S(1)}, bf16[4,32,1024]{2,1,0:T(8,128)(2,1)}, f32[4,32,1024]{2,1,0:T(8,128)}, f...) conditional(s32[]{:T(128)} %convert_element_type.293, (bf16[32,1024]{1,0:T(8,128)(2,1)S(1)}, ...), branch_computations={%region_2.3_spmd, %region_3.6_spmd} | conditional | flops 806912000 | bytes 45040972 | solution.py:171
  183.5 5.0 fusion.12
  188.5 11.3 %copy.18 = bf16[1024,4096]{1,0:T(8,128)(2,1)} copy(bf16[1024,4096]{0,1:T(8,128)(2,1)} %get-tuple-element.2592) | data formatting | bytes 16777216 | tf_op jit(solution)/shard_map
  199.7 11.9 %while.257 = (s32[]{:T(128)}, bf16[32,1024]{1,0:T(8,128)(2,1)S(1)}, f32[32,1024]{1,0:T(8,128)S(1)}, bf16[2,32,1024]{2,1,0:T(8,128)(2,1)}, f32[2,32,1024]{2,1,0:T...) while((s32[]{:T(128)}, bf16[32,1024]{1,0:T(8,128)(2,1)S(1)}, ...), condition=%wide.region_5.5_spmd, body=%wide.region_4.4_spmd.sunk | while | flops 269713408 | bytes 12780137 | solution.py:59
  199.7 4.9 convolution_add_fusion.14
  205.7 4.9 convolution_add_fusion.14
  212.3 1.6 constant_dynamic-update-slice_fusion.2
  213.9 1.5 broadcast_in_dim.111
  220.5 31.6 %conditional.15 = (bf16[32,1024]{1,0:T(8,128)(2,1)S(1)}, f32[32,1024]{1,0:T(8,128)S(1)}, bf16[4,32,1024]{2,1,0:T(8,128)(2,1)}, f32[4,32,1024]{2,1,0:T(8,128)}, f...) conditional(s32[]{:T(128)} %convert_element_type.292, (bf16[32,1024]{1,0:T(8,128)(2,1)S(1)}, ...), branch_computations={%region_6.7_spmd, %region_7.10_spmd} | conditional | flops 806912000 | bytes 43270992 | solution.py:171
  220.5 11.3 %copy.19 = bf16[1024,4096]{1,0:T(8,128)(2,1)} copy(bf16[1024,4096]{0,1:T(8,128)(2,1)} %get-tuple-element.2601) | data formatting | bytes 16777216 | tf_op jit(solution)/shard_map
  231.8 4.9 fusion.31
  236.8 11.9 %while.258 = (s32[]{:T(128)}, bf16[32,1024]{1,0:T(8,128)(2,1)S(1)}, f32[32,1024]{1,0:T(8,128)S(1)}, bf16[2,32,1024]{2,1,0:T(8,128)(2,1)}, f32[2,32,1024]{2,1,0:T...) while((s32[]{:T(128)}, bf16[32,1024]{1,0:T(8,128)(2,1)S(1)}, ...), condition=%wide.region_9.9_spmd, body=%wide.region_8.8_spmd.sunk | while | flops 269713408 | bytes 12780137 | solution.py:59
  236.8 4.9 convolution_add_fusion.13
  242.8 4.9 convolution_add_fusion.13
  248.7 1.6 constant_dynamic-update-slice_fusion.5
  252.1 2.2 collective-permute-start.1
  256.2 33.8 %collective-permute-start.2 = (bf16[2,32,1024]{2,1,0:T(8,128)(2,1)}, bf16[2,32,1024]{2,1,0:T(8,128)(2,1)S(1)}, u32[]{:S(2)}, u32[]{:S(2)}) collective-permute-start(bf16[2,32,1024]{2,1,0:T(8,128)(2,1)} %get-tuple-element.2496), channel_id=1, source_target_pairs={{0,64},{64,128},{128,192},{1,65},{65,129},{129,193},{2,66},{66,130... | collective-permute-start | bytes 393224 | tf_op jit(solution)/shard_map/ppermute | solution.py:31
  292.1 5.3 collective-permute-start.3
  301.5 3.1 conditional.19
  305.9 36.0 %collective-permute-done.4 = bf16[2,32,1024]{2,1,0:T(8,128)(2,1)S(1)} collective-permute-done((bf16[2,32,1024]{2,1,0:T(8,128)(2,1)}, bf16[2,32,1024]{2,1,0:T(8,128)(2,1)S(1)}, u32[]{:S(2)}, u32[]{:S(2)}) %collective-permute-start.4) | collective-permute-done | bytes 131104 | tf_op jit(solution)/shard_map/ppermute | solution.py:31
  341.8 8.8 %conditional.20 = (f32[32,1024]{1,0:T(8,128)}, f32[32,1024]{1,0:T(8,128)}, bf16[4,32,4096]{2,1,0:T(8,128)(2,1)}, bf16[2,32,1024]{2,1,0:T(8,128)(2,1)}) conditional(s32[]{:T(128)} %convert_element_type.290, (f32[32,1024]{1,0:T(8,128)}, f32[32,1024]{1,0:T(8,128)}, bf16[4,32,4096]{2,1,0:T(8,128)(2,1)}) %tuple.301, (pred[]{:T(512)}, ...), branch_computations={%region_28.29_spmd, %region_29.34_spmd} | conditional | flops 807567360 | bytes 43976584 | solution.py:220
  351.9 5.8 collective-permute-done.5
  359.7 141.5 %collective-permute-done.6 = bf16[2,32,1024]{2,1,0:T(8,128)(2,1)S(1)} collective-permute-done((bf16[2,32,1024]{2,1,0:T(8,128)(2,1)}, bf16[2,32,1024]{2,1,0:T(8,128)(2,1)S(1)}, u32[]{:S(2)}, u32[]{:S(2)}) %collective-permute-start.6) | collective-permute-done | bytes 131104 | tf_op jit(solution)/shard_map/ppermute | solution.py:31
  501.2 33.0 %conditional.22 = (f32[32,1024]{1,0:T(8,128)}, f32[32,1024]{1,0:T(8,128)}, bf16[4,32,4096]{2,1,0:T(8,128)(2,1)}, bf16[2,32,1024]{2,1,0:T(8,128)(2,1)}) conditional(s32[]{:T(128)} %convert_element_type.292, (f32[32,1024]{1,0:T(8,128)}, f32[32,1024]{1,0:T(8,128)}, bf16[4,32,4096]{2,1,0:T(8,128)(2,1)}) %tuple.305, (pred[]{:T(512)}, ...), branch_computations={%region_40.41_spmd, %region_41.46_spmd} | conditional | flops 807567360 | bytes 43976584 | solution.py:220
  503.5 11.7 %copy.26 = bf16[1024,4096]{1,0:T(8,128)(2,1)} copy(bf16[1024,4096]{0,1:T(8,128)(2,1)} %get-tuple-element.2694) | data formatting | bytes 16777216 | tf_op jit(solution)/shard_map
  515.3 17.4 %while.264 = (s32[]{:T(128)}, f32[32,1024]{1,0:T(8,128)}, f32[32,1024]{1,0:T(8,128)}, bf16[2,32,4096]{2,1,0:T(8,128)(2,1)S(1)}, bf16[2,32,1024]{2,1,0:T(8,128)(2...) while((s32[]{:T(128)}, f32[32,1024]{1,0:T(8,128)}, ...), condition=%wide.region_43.43_spmd, body=%wide.region_42.42_spmd.sunk | while | flops 270565376 | bytes 13042829 | solution.py:102
  515.3 1.7 multiply_multiply_fusion.11
  517.2 6.6 %fusion.275 = f32[32,1024]{1,0:T(8,128)} fusion(bf16[1024,4096]{1,0:T(8,128)(2,1)} %get-tuple-element.3734, f32[32,1024]{1,0:T(8,128)S(1)} %get-tuple-element.3536, f32[32,1024]{1,0:T(8,128)S(1)} %get-tuple-element.3538, f32[32,1024]{1,0:T(8,128)S(1)} %get-tuple-element.3539, f32[32,1024]{1,0:T(8,128)S(1)} %get-tuple-element.3540, f32[32]{0:T(128)S(1)} %fusion.274), kind=kOutput, calls=%fused_computation.219.clone.1 | convolution fusion | flops 269090816 | bytes 9044096 | tf_op jit(solution)/shard_map/cond/branch_1_fun/while/body/eval_jaxpr/dot_general | solution.py:66
  523.9 1.7 multiply_multiply_fusion.11
  525.8 6.9 %fusion.275 = f32[32,1024]{1,0:T(8,128)} fusion(bf16[1024,4096]{1,0:T(8,128)(2,1)} %get-tuple-element.3734, f32[32,1024]{1,0:T(8,128)S(1)} %get-tuple-element.3536, f32[32,1024]{1,0:T(8,128)S(1)} %get-tuple-element.3538, f32[32,1024]{1,0:T(8,128)S(1)} %get-tuple-element.3539, f32[32,1024]{1,0:T(8,128)S(1)} %get-tuple-element.3540, f32[32]{0:T(128)S(1)} %fusion.274), kind=kOutput, calls=%fused_computation.219.clone.1 | convolution fusion | flops 269090816 | bytes 9044096 | tf_op jit(solution)/shard_map/cond/branch_1_fun/while/body/eval_jaxpr/dot_general | solution.py:66
  535.5 14.8 %collective-permute-done.7 = bf16[2,32,1024]{2,1,0:T(8,128)(2,1)S(1)} collective-permute-done((bf16[2,32,1024]{2,1,0:T(8,128)(2,1)}, bf16[2,32,1024]{2,1,0:T(8,128)(2,1)S(1)}, u32[]{:S(2)}, u32[]{:S(2)}) %collective-permute-start.7) | collective-permute-done | bytes 131104 | tf_op jit(solution)/shard_map/ppermute | solution.py:31
  550.3 32.1 %conditional.23 = (bf16[4,32,4096]{2,1,0:T(8,128)(2,1)}) conditional(s32[]{:T(128)} %convert_element_type.298, bf16[4,32,4096]{2,1,0:T(8,128)(2,1)} %get-tuple-element.2518, (pred[]{:T(512)}, s32[]{:T(128)}, bf16[4,32,1024]{2,1,0:T(8,128)(2,1)S(1)}, bf16[2,32,1024]{2,1,0:T(8,128)(2,1)S(1)}, f32[4,32,1024]{2,1,0:T(8,128)}, ...), branch_computations={%region_46.47_spmd, %region_47.50_spmd} | conditional | flops 270630912 | bytes 34932592 | solution.py:220
  551.3 1.3 constant_dynamic-slice_fusion.19
  552.7 11.5 %copy.27 = bf16[1024,4096]{1,0:T(8,128)(2,1)} copy(bf16[1024,4096]{0,1:T(8,128)(2,1)} %get-tuple-element.2708) | data formatting | bytes 16777216 | tf_op jit(solution)/shard_map
  564.2 17.1 %while.265 = (s32[]{:T(128)}, f32[32,1024]{1,0:T(8,128)}, f32[32,1024]{1,0:T(8,128)}, bf16[2,32,4096]{2,1,0:T(8,128)(2,1)S(1)}, bf16[2,32,1024]{2,1,0:T(8,128)(2...) while((s32[]{:T(128)}, f32[32,1024]{1,0:T(8,128)}, ...), condition=%wide.region_49.49_spmd, body=%wide.region_48.48_spmd.sunk | while | flops 270565376 | bytes 13042829 | solution.py:102
  564.3 1.7 multiply_multiply_fusion.10
  566.2 6.6 %fusion.270 = f32[32,1024]{1,0:T(8,128)} fusion(bf16[1024,4096]{1,0:T(8,128)(2,1)} %get-tuple-element.3701, f32[32,1024]{1,0:T(8,128)S(1)} %get-tuple-element.3520, f32[32,1024]{1,0:T(8,128)S(1)} %get-tuple-element.3522, f32[32,1024]{1,0:T(8,128)S(1)} %get-tuple-element.3523, f32[32,1024]{1,0:T(8,128)S(1)} %get-tuple-element.3524, f32[32]{0:T(128)S(1)} %fusion.269), kind=kOutput, calls=%fused_computation.254.clone.1 | convolution fusion | flops 269090816 | bytes 9044096 | tf_op jit(solution)/shard_map/cond/branch_1_fun/while/body/eval_jaxpr/dot_general | solution.py:66
  572.9 1.7 multiply_multiply_fusion.10
  574.7 6.6 %fusion.270 = f32[32,1024]{1,0:T(8,128)} fusion(bf16[1024,4096]{1,0:T(8,128)(2,1)} %get-tuple-element.3701, f32[32,1024]{1,0:T(8,128)S(1)} %get-tuple-element.3520, f32[32,1024]{1,0:T(8,128)S(1)} %get-tuple-element.3522, f32[32,1024]{1,0:T(8,128)S(1)} %get-tuple-element.3523, f32[32,1024]{1,0:T(8,128)S(1)} %get-tuple-element.3524, f32[32]{0:T(128)S(1)} %fusion.269), kind=kOutput, calls=%fused_computation.254.clone.1 | convolution fusion | flops 269090816 | bytes 9044096 | tf_op jit(solution)/shard_map/cond/branch_1_fun/while/body/eval_jaxpr/dot_general | solution.py:66
  582.4 3.3 all_to_all.14
  585.7 2.2 copy.28
  587.9 27.1 %all_to_all.19 = bf16[128,64,64]{0,2,1:T(8,128)(2,1)S(1)} all-to-all(bf16[128,64,64]{0,2,1:T(8,128)(2,1)S(1)} %copy.28), channel_id=1, replica_groups=mesh['section_0'=2,'section_1'=2,'dp'=64] {'dp'}, dimensions={1} | all-to-all | bytes 2097152 | tf_op jit(solution)/shard_map/all_to_all | solution.py:229
  615.8 9.5 %convolution_bitcast_fusion = f32[1,1024,64]{1,2,0:T(8,128)} fusion(bf16[8192,1024]{1,0:T(8,128)(2,1)} %all-gather.4.cloned.1.call-done, bf16[128,64,64]{0,2,1:T(8,128)(2,1)S(1)} %all_to_all.19), kind=kOutput, calls=%fused_computation.323 | convolution fusion | flops 1073741824 | bytes 18087936 | tf_op jit(solution)/shard_map/dot_general | solution.py:230
  (109 shorter events, 41.5 us)
Async XLA Ops:
  8.0 19.3 %reduce-scatter.3.cloned.1.call-start = ((), (), s32[]{:S(2)}) async-start(), calls=%async_computation.3 | async-start | bytes 786432 | tf_op jit(solution)/shard_map/reduce_scatter | solution.py:24
  10.7 37.3 %reduce-scatter.5.cloned.1.call-start = ((), (), s32[]{:S(2)}) async-start(), calls=%async_computation.4 | async-start | bytes 393216 | tf_op jit(solution)/shard_map/reduce_scatter | solution.py:25
  27.3 156.1 %all-gather.6.cloned.1.call-start = ((), (), s32[]{:S(2)}) async-start(), calls=%async_computation.6 | async-start | bytes 8519680 | tf_op jit(solution)/shard_map/all_gather | solution.py:135
  27.9 587.9 %all-gather.4.cloned.1.call-start = ((), (), s32[]{:S(2)}) async-start(), calls=%async_computation.5 | async-start | bytes 17039360 | tf_op jit(solution)/shard_map/all_gather | solution.py:231
  218.1 2.5 collective-permute-start
  220.5 11.3 %copy-start = (bf16[4,32,1024]{2,1,0:T(8,128)(2,1)S(1)}, bf16[4,32,1024]{2,1,0:T(8,128)(2,1)}, u32[]{:S(2)}) copy-start(bf16[4,32,1024]{2,1,0:T(8,128)(2,1)} %get-tuple-element.2179) | copy-start | bytes 786436 | tf_op jit(solution)/shard_map/cond
  220.5 11.3 %copy-start.4 = (f32[1,4096]{1,0:T(1,128)S(1)}, f32[1,4096]{1,0:T(1,128)}, u32[]{:S(2)}) copy-start(f32[1,4096]{1,0:T(1,128)} %get-tuple-element.2183) | copy-start | bytes 49156 | tf_op jit(solution)/shard_map/cond
  252.1 3.4 collective-permute-start.1
  256.2 35.0 %collective-permute-start.2 = (bf16[2,32,1024]{2,1,0:T(8,128)(2,1)}, bf16[2,32,1024]{2,1,0:T(8,128)(2,1)S(1)}, u32[]{:S(2)}, u32[]{:S(2)}) collective-permute-start(bf16[2,32,1024]{2,1,0:T(8,128)(2,1)} %get-tuple-element.2496), channel_id=1, source_target_pairs={{0,64},{64,128},{128,192},{1,65},{65,129},{129,193},{2,66},{66,130... | collective-permute-start | bytes 393224 | tf_op jit(solution)/shard_map/ppermute | solution.py:31
  292.1 6.5 %collective-permute-start.3 = (bf16[2,32,1024]{2,1,0:T(8,128)(2,1)}, bf16[2,32,1024]{2,1,0:T(8,128)(2,1)S(1)}, u32[]{:S(2)}, u32[]{:S(2)}) collective-permute-start(bf16[2,32,1024]{2,1,0:T(8,128)(2,1)} %get-tuple-element.2500), channel_id=1, source_target_pairs={{0,64},{64,128},{128,192},{1,65},{65,129},{129,193},{2,66},{66,130... | collective-permute-start | bytes 393224 | tf_op jit(solution)/shard_map/ppermute | solution.py:31
  298.5 1.1 copy-start.6
  298.5 1.8 copy-start.7
  298.5 1.9 copy-start.8
  298.5 1.9 copy-start.3
  298.5 3.0 copy-start.2
  304.6 37.2 %collective-permute-start.4 = (bf16[2,32,1024]{2,1,0:T(8,128)(2,1)}, bf16[2,32,1024]{2,1,0:T(8,128)(2,1)S(1)}, u32[]{:S(2)}, u32[]{:S(2)}) collective-permute-start(bf16[2,32,1024]{2,1,0:T(8,128)(2,1)} %get-tuple-element.2509), channel_id=1, source_target_pairs={{64,0},{128,64},{192,128},{65,1},{129,65},{193,129},{66,2},{130,66... | collective-permute-start | bytes 393224 | tf_op jit(solution)/shard_map/ppermute | solution.py:31
  350.6 7.1 %collective-permute-start.5 = (bf16[2,32,1024]{2,1,0:T(8,128)(2,1)}, bf16[2,32,1024]{2,1,0:T(8,128)(2,1)S(1)}, u32[]{:S(2)}, u32[]{:S(2)}) collective-permute-start(bf16[2,32,1024]{2,1,0:T(8,128)(2,1)} %get-tuple-element.2513), channel_id=1, source_target_pairs={{64,0},{128,64},{192,128},{65,1},{129,65},{193,129},{66,2},{130,66... | collective-permute-start | bytes 393224 | tf_op jit(solution)/shard_map/ppermute | solution.py:31
  358.4 142.7 %collective-permute-start.6 = (bf16[2,32,1024]{2,1,0:T(8,128)(2,1)}, bf16[2,32,1024]{2,1,0:T(8,128)(2,1)S(1)}, u32[]{:S(2)}, u32[]{:S(2)}) collective-permute-start(bf16[2,32,1024]{2,1,0:T(8,128)(2,1)} %get-tuple-element.2517), channel_id=1, source_target_pairs={{64,0},{128,64},{192,128},{65,1},{129,65},{193,129},{66,2},{130,66... | collective-permute-start | bytes 393224 | tf_op jit(solution)/shard_map/ppermute | solution.py:31
  534.2 16.1 %collective-permute-start.7 = (bf16[2,32,1024]{2,1,0:T(8,128)(2,1)}, bf16[2,32,1024]{2,1,0:T(8,128)(2,1)S(1)}, u32[]{:S(2)}, u32[]{:S(2)}) collective-permute-start(bf16[2,32,1024]{2,1,0:T(8,128)(2,1)} %get-tuple-element.2519), channel_id=1, source_target_pairs={{64,0},{128,64},{192,128},{65,1},{129,65},{193,129},{66,2},{130,66... | collective-permute-start | bytes 393224 | tf_op jit(solution)/shard_map/ppermute | solution.py:31
Sparse Core Ops, SparseCore 0:
  11.3 15.9 reduce-scatter.2
  29.9 18.0 reduce-scatter.4
Sparse Core Ops, SparseCore 1:
  31.3 152.1 all-gather.5
  300.5 267.5 all-gather.3
where the time goes:
time: 640 us; the launch traced here: 633 us
  waiting for transfers between devices  374 us (58%)
  local copies, waits for them, and re-layouts  75.1 us (12%)
  matrix products  65.9 us (10%)
  starting transfers between devices  47.9 us (7%)
  blocking collectives  27.1 us (4%)
  other arithmetic  18.4 us (3%)
  between operations  16 us (2%)
  loops' own time  8.9 us (1%)
    ppermute x8, waiting for transfers between devices, from_behind(): return lax.ppermute(array, axis, pairs)  203 us
    all_gather x1, waiting for transfers between devices, on_device(): w_rec = lax.all_gather(w_recurrent[0], 'dp', axis=1, tiled=True)  134 us
    another operation x15, local copies, waits for them, and re-layouts  51.2 us
    ppermute x8, starting transfers between devices, from_behind(): return lax.ppermute(array, axis, pairs)  47.7 us
    all_to_all x1, blocking collectives, on_device(): lax.all_to_all(gate_rows, 'dp', split_axis=1, concat_axis=0, tiled=True)  27.1 us
    dot_general x4, matrix products, times_transposed(): lax.dot_general(operand, matrix, (((1,), (1,)), ((), ())), preferred_elem...  26.8 us
    reduce_scatter x1, waiting for transfers between devices, scatter_pairs(): return lax.psum_scatter(parts, chips, scatter_dimension=0, tiled=True)[0]  20 us
    dot_general x4, matrix products, advance(): jnp.dot(hidden_prev, w_rec, preferred_element_type=jnp.float32)  19.7 us
  transfers between devices with their start and end apart: 12, of which 11 were waited for; matrix products, arithmetic and copies ran while one was open for 12% of the time, Pallas kernels for 0%

commit v1 on v0

v1 whole, which is shorter than its diff:
```python
import jax
import jax.numpy as jnp
from jax import lax
from jax.experimental import pallas as pl
from jax.experimental.pallas import tpu as pltpu
from jax.sharding import Mesh
from jax.sharding import PartitionSpec as P

S, Z, X, Y = 4, 8, 2, 4
STEPS = 4
ROWS = 32
D = 1024
LANES = 128
GATES = 4
ALL_ROWS = Y * ROWS
LOCAL = GATES * 2 * LANES
MESH = pl.DeviceIdType.MESH
BF16 = jnp.bfloat16
F32 = jnp.float32


def sigmoid(v):
    return 0.5 * jnp.tanh(0.5 * v) + 0.5


def nt_dot(a, b):
    return lax.dot_general(a, b, (((1,), (1,)), ((), ())), preferred_element_type=F32)


def nn_dot(a, b):
    return jnp.dot(a, b, preferred_element_type=F32)


def remote(src, dst, send_sem, recv_sem, where):
    return pltpu.make_async_remote_copy(
        src_ref=src,
        dst_ref=dst,
        send_sem=send_sem,
        recv_sem=recv_sem,
        device_id=where,
        device_id_type=MESH,
    )


def kernel(
    obs_ref, cot_ref, win_hbm, wrt_hbm, bias_ref, st_hbm, info_ref,
    hid_out, dw_out, db_out,
    info, st, win, wrt, xb, hb, eb, cot_st, c_st, c_in, cells, gates, acc, live,
    grads, grads_t, carry, a_send, a_recv, g_send, g_recv, e_send, hmat, dbs, db_in,
    dw_send, dw_recv, hid_st,
    info_ss, info_rs, st_ss, st_rs, st_ls, wa_ss, wa_rs, wa_ls, ring_ss, ring_rs, win_ls,
    obs_ss, obs_rs, cot_ss, cot_rs, c_ss, c_rs, h_ss, h_rs, x_ss, x_rs,
    a_ss, a_rs, g_ss, g_rs, e_ss, e_rs, dw_ss, dw_rs, db_ss, db_rs, hid_ls,
):
    s = lax.axis_index("s")
    z = lax.axis_index("z")
    x = lax.axis_index("x")
    y = lax.axis_index("y")
    up_y = [lax.rem(y + k, Y) for k in range(1, Y)]
    down_y = [lax.rem(y + Y - k, Y) for k in range(1, Y)]
    up_s = [lax.rem(s + k, S) for k in range(1, S)]
    down_s = [lax.rem(s + S - k, S) for k in range(1, S)]
    z_up, z_down = lax.rem(z + 1, Z), lax.rem(z + Z - 1, Z)
    own_half = lax.rem(y, 2)
    user_y = 2 * x + y // 2
    owner_x = y // 2
    owner_y = [2 * own_half + p for p in range(2)]

    def is_me(zz, xx, yy):
        return (zz == z) & (xx == x) & (yy == y)

    barrier = pltpu.get_barrier_semaphore()

    def greet(where):
        pl.semaphore_signal(barrier, inc=1, device_id=where, device_id_type=MESH)

    for k in range(Y - 1):
        greet({"y": down_y[k]})
    for k in range(S - 1):
        greet({"s": down_s[k]})
    greet({"z": z_up})
    greet({"z": z_down})
    for p in range(2):
        @pl.when(jnp.logical_not(is_me(z, owner_x, owner_y[p])))
        def _():
            greet({"x": owner_x, "y": owner_y[p]})

    @pl.loop(0, Z)
    def _(zz):
        for xx in range(X):
            @pl.when(jnp.logical_not(is_me(zz, xx, user_y)))
            def _():
                greet({"z": zz, "x": xx, "y": user_y})

    mine = is_me(z, owner_x, owner_y[0]) | is_me(z, owner_x, owner_y[1])
    base = (Y - 1) + (S - 1) + 2 + X + Z * 2
    pl.semaphore_wait(barrier, jnp.where(mine, base - 2, base))

    def first_hop(xx):
        return remote(
            wrt_hbm, wrt.at[z, own_half], wa_ss.at[xx], wa_rs.at[own_half],
            {"x": xx, "y": user_y},
        )

    own_copy = pltpu.make_async_copy(wrt_hbm, wrt.at[z, own_half], wa_ls)
    for xx in range(X):
        @pl.when(is_me(z, xx, user_y))
        def _():
            own_copy.start()

        @pl.when(jnp.logical_not(is_me(z, xx, user_y)))
        def _():
            first_hop(xx).start()

    def st_copy(k):
        return remote(st_hbm.at[up_s[k]], st.at[s], st_ss.at[k], st_rs.at[k], {"s": up_s[k]})

    def st_arrival(k):
        return remote(
            st.at[down_s[k]], st.at[down_s[k]], st_ss.at[k], st_rs.at[k], {"s": up_s[k]}
        )

    for k in range(S - 1):
        st_copy(k).start()
    st_own = pltpu.make_async_copy(st_hbm.at[s], st.at[s], st_ls)
    st_own.start()

    def win_copy(gate, half):
        first = pl.multiple_of(gate * D + half * Y * LANES + y * LANES, LANES)
        block = gate * 2 + half
        return pltpu.make_async_copy(
            win_hbm.at[:, pl.ds(first, LANES)],
            win.at[:, pl.ds(block * LANES, LANES)],
            win_ls.at[block],
        )

    for gate in range(GATES):
        for half in range(2):
            win_copy(gate, half).start()

    info[y] = info_ref[...]

    def info_copy(k):
        return remote(info.at[y], info.at[y], info_ss.at[k], info_rs.at[k], {"y": up_y[k]})

    def info_arrival(k):
        return remote(
            info.at[down_y[k]], info.at[down_y[k]], info_ss.at[k], info_rs.at[k], {"y": up_y[k]}
        )

    for k in range(Y - 1):
        info_copy(k).start()

    def obs_copy(k):
        return remote(
            xb.at[:, :, :, y], xb.at[:, :, :, y], obs_ss.at[k], obs_rs.at[k], {"y": up_y[k]}
        )

    def obs_arrival(k):
        part = xb.at[:, :, :, down_y[k]]
        return remote(part, part, obs_ss.at[k], obs_rs.at[k], {"y": up_y[k]})

    @pl.when(s == 0)
    def _():
        for t in range(STEPS):
            for half in range(2):
                for yy in range(Y):
                    first = (half * Y + yy) * LANES
                    xb[t, half, yy, y] = obs_ref[t, :, first : first + LANES]
        for k in range(Y - 1):
            obs_copy(k).start()

    def cot_copy(k):
        return remote(
            cot_st.at[up_y[k]], eb.at[:, :, y], cot_ss.at[k], cot_rs.at[k], {"y": up_y[k]}
        )

    def cot_arrival(k):
        part = eb.at[:, :, down_y[k]]
        return remote(part, part, cot_ss.at[k], cot_rs.at[k], {"y": up_y[k]})

    @pl.when(s == S - 1)
    def _():
        for t in range(STEPS):
            for half in range(2):
                for yy in range(Y):
                    first = (half * Y + yy) * LANES
                    cot_st[yy, t, half] = cot_ref[t, :, first : first + LANES]
        for t in range(STEPS):
            for half in range(2):
                eb[t, half, y] = cot_st[y, t, half]
        for k in range(Y - 1):
            cot_copy(k).start()

    def ring_up(step):
        part = wrt.at[lax.rem(z + Z - step, Z)]
        if step == Z // 2 - 1:
            part = part.at[0]
        return remote(part, part, ring_ss.at[0, step], ring_rs.at[0, step], {"z": z_up})

    def ring_down(step):
        part = wrt.at[lax.rem(z + step, Z)]
        if step == Z // 2 - 1:
            part = part.at[1]
        return remote(part, part, ring_ss.at[1, step], ring_rs.at[1, step], {"z": z_down})

    def ring_wait(step):
        from_down = wrt.at[lax.rem(z + Z - 1 - step, Z)]
        from_up = wrt.at[lax.rem(z + 1 + step, Z)]
        if step == Z // 2 - 1:
            from_down = from_down.at[0]
            from_up = from_up.at[1]
        remote(
            from_down, from_down, ring_ss.at[0, step], ring_rs.at[0, step], {"z": z_up}
        ).wait_recv()
        remote(
            from_up, from_up, ring_ss.at[1, step], ring_rs.at[1, step], {"z": z_down}
        ).wait_recv()

    for p in range(2):
        @pl.when(is_me(z, owner_x, owner_y[p]))
        def _():
            own_copy.wait()

        @pl.when(jnp.logical_not(is_me(z, owner_x, owner_y[p])))
        def _():
            part = wrt.at[z, p]
            remote(
                part, part, wa_ss.at[0], wa_rs.at[p], {"x": owner_x, "y": owner_y[p]}
            ).wait_recv()

    ring_up(0).start()
    ring_down(0).start()

    st_own.wait()
    for k in range(S - 1):
        st_arrival(k).wait_recv()
    marks = info[y]
    chosen = jnp.zeros((ROWS, 2 * D), F32)
    for owner in range(S):
        here = marks[:, STEPS + owner : STEPS + owner + 1] > 0.5
        chosen = chosen + jnp.where(here, st[owner].astype(F32), 0.0)
    for half in range(2):
        for yy in range(Y):
            first = (half * Y + yy) * LANES
            hb[0, half, yy, y] = chosen[:, first : first + LANES].astype(BF16)
            c_st[yy, half] = chosen[:, D + first : D + first + LANES].astype(BF16)
    c_in[y] = c_st[y]

    def h0_copy(k):
        part = hb.at[0, :, :, y]
        return remote(part, part, h_ss.at[0, k], h_rs.at[0, k], {"y": up_y[k]})

    def h0_arrival(k):
        part = hb.at[0, :, :, down_y[k]]
        return remote(part, part, h_ss.at[0, k], h_rs.at[0, k], {"y": up_y[k]})

    def c0_copy(k):
        return remote(c_st.at[up_y[k]], c_in.at[y], c_ss.at[k], c_rs.at[k], {"y": up_y[k]})

    def c0_arrival(k):
        part = c_in.at[down_y[k]]
        return remote(part, part, c_ss.at[k], c_rs.at[k], {"y": up_y[k]})

    for k in range(Y - 1):
        h0_copy(k).start()
        c0_copy(k).start()

    ring_wait(0)
    ring_up(1).start()
    ring_down(1).start()

    for k in range(Y - 1):
        info_arrival(k).wait_recv()
        c0_arrival(k).wait_recv()
    marks_all = info[...].reshape(ALL_ROWS, LANES)
    for t in range(STEPS):
        live[t] = jnp.broadcast_to(marks_all[:, t : t + 1], (ALL_ROWS, LANES))
    for half in range(2):
        cells[0, half] = c_in[:, half].reshape(ALL_ROWS, LANES).astype(F32)
    for gate in range(GATES):
        for half in range(2):
            win_copy(gate, half).wait()

    ring_wait(1)
    ring_up(2).start()
    ring_down(2).start()

    @pl.when(s == 0)
    def _():
        for k in range(Y - 1):
            obs_arrival(k).wait_recv()

    @pl.when(s == S - 1)
    def _():
        for k in range(Y - 1):
            cot_arrival(k).wait_recv()

    for k in range(Y - 1):
        h0_arrival(k).wait_recv()

    ring_wait(2)
    ring_up(3).start()
    ring_down(3).start()
    ring_wait(3)

    def whole(ref, t):
        return jnp.concatenate(
            [
                ref[t, half, yy].reshape(ALL_ROWS, LANES)
                for half in range(2)
                for yy in range(Y)
            ],
            axis=1,
        )

    def h_copy(t, k):
        part = hb.at[t, :, y]
        return remote(part, part, h_ss.at[t, k], h_rs.at[t, k], {"y": up_y[k]})

    def h_arrival(t, k):
        part = hb.at[t, :, down_y[k]]
        return remote(part, part, h_ss.at[t, k], h_rs.at[t, k], {"y": up_y[k]})

    def x_copy(t):
        return remote(hb.at[t + 1], xb.at[t], x_ss.at[t], x_rs.at[t], {"s": up_s[0]})

    def x_arrival(t):
        return remote(xb.at[t], xb.at[t], x_ss.at[t], x_rs.at[t], {"s": up_s[0]})

    def pass_up(t):
        for k in range(Y - 1):
            h_arrival(t + 1, k).wait_recv()

        @pl.when(s < S - 1)
        def _():
            x_copy(t).start()

    def project(t):
        inputs = whole(xb, t)
        for gate in range(GATES):
            columns = slice(gate * 2 * LANES, (gate + 1) * 2 * LANES)
            part = nn_dot(inputs, win[:, columns])
            for half in range(2):
                first = pl.multiple_of(gate * D + half * Y * LANES + y * LANES, LANES)
                acc[gate, half] = (
                    part[:, half * LANES : (half + 1) * LANES] + bias_ref[:, pl.ds(first, LANES)]
                )

    @pl.loop(0, STEPS)
    def _(t):
        @pl.when(s == 0)
        def _():
            project(t)

        @pl.when(t > 0)
        def _():
            pass_up(t - 1)

        @pl.when(s > 0)
        def _():
            x_arrival(t).wait_recv()
            project(t)

        before = whole(hb, t)
        for gate in range(GATES):
            rows = wrt[2 * gate : 2 * gate + 2].reshape(2 * LANES, D)
            part = nt_dot(before, rows)
            for half in range(2):
                pre = acc[gate, half] + part[:, half * LANES : (half + 1) * LANES]
                gates[t, gate, half] = jnp.tanh(pre) if gate == 2 else sigmoid(pre)
        for half in range(2):
            cell = (
                gates[t, 1, half] * cells[t, half] + gates[t, 0, half] * gates[t, 2, half]
            )
            cells[t + 1, half] = cell
            hidden = (gates[t, 3, half] * jnp.tanh(cell)).astype(BF16)
            hb[t + 1, half, y] = hidden.reshape(Y, ROWS, LANES)
        for k in range(Y - 1):
            h_copy(t + 1, k).start()

    pass_up(STEPS - 1)
    for t in range(STEPS):
        for half in range(2):
            for yy in range(Y):
                first = (half * Y + yy) * LANES
                hid_st[t, :, first : first + LANES] = hb[t + 1, half, yy, y]
    hid_copy = pltpu.make_async_copy(hid_st, hid_out, hid_ls)
    hid_copy.start()
    for t in range(STEPS):
        hmat[t * ALL_ROWS : (t + 1) * ALL_ROWS, :] = whole(hb, t)

    carry[...] = jnp.zeros_like(carry)
    dbs[...] = jnp.zeros_like(dbs)

    def a_copy(t, k):
        return remote(
            a_send.at[t, up_y[k]], a_recv.at[t, y], a_ss.at[t, k], a_rs.at[t, k], {"y": up_y[k]}
        )

    def a_arrival(t, k):
        part = a_recv.at[t, down_y[k]]
        return remote(part, part, a_ss.at[t, k], a_rs.at[t, k], {"y": up_y[k]})

    def g_copy(t, k):
        return remote(
            g_send.at[t, up_y[k]], g_recv.at[t, y], g_ss.at[t, k], g_rs.at[t, k], {"y": up_y[k]}
        )

    def g_arrival(t, k):
        part = g_recv.at[t, down_y[k]]
        return remote(part, part, g_ss.at[t, k], g_rs.at[t, k], {"y": up_y[k]})

    def e_copy(t):
        return remote(e_send.at[t], eb.at[t], e_ss.at[t], e_rs.at[t], {"s": down_s[0]})

    def e_arrival(t):
        return remote(eb.at[t], eb.at[t], e_ss.at[t], e_rs.at[t], {"s": down_s[0]})

    def total(sent, received, t, half):
        value = sent[t, y, half].astype(F32)
        for k in range(Y - 1):
            value = value + received[t, down_y[k], half].astype(F32)
        return value

    @pl.loop(0, STEPS)
    def _(back):
        t = STEPS - 1 - back

        @pl.when(s < S - 1)
        def _():
            e_arrival(t).wait_recv()

        for half in range(2):
            acc[0, half] = eb[t, half].reshape(ALL_ROWS, LANES).astype(F32)

        @pl.when(back > 0)
        def _():
            for k in range(Y - 1):
                a_arrival(t + 1, k).wait_recv()
            for half in range(2):
                acc[0, half] = acc[0, half] + total(a_send, a_recv, t + 1, half)

        for half in range(2):
            in_gate = gates[t, 0, half]
            forget = gates[t, 1, half]
            candidate = gates[t, 2, half]
            out_gate = gates[t, 3, half]
            alive = live[t]
            total_h = acc[0, half]
            squashed = jnp.tanh(cells[t + 1, half])
            total_c = carry[half] + total_h * out_gate * (1.0 - squashed * squashed)
            parts = (
                total_c * candidate * in_gate * (1.0 - in_gate) * alive,
                total_c * cells[t, half] * forget * (1.0 - forget) * alive,
                total_c * in_gate * (1.0 - candidate * candidate) * alive,
                total_h * squashed * out_gate * (1.0 - out_gate) * alive,
            )
            carry[half] = total_c * forget * alive
            for gate in range(GATES):
                grads[2 * gate + half] = parts[gate].astype(BF16)

        gate_grads = jnp.concatenate([grads[block] for block in range(2 * GATES)], axis=1)

        @pl.when(t > 0)
        def _():
            for j in range(4):
                columns = slice(j * 2 * LANES, (j + 1) * 2 * LANES)
                part = nn_dot(
                    gate_grads, wrt[:, :, :, columns].reshape(LOCAL, 2 * LANES)
                ).astype(BF16)
                for n in range(2):
                    block = 2 * j + n
                    a_send[t, block % Y, block // Y] = part[:, n * LANES : (n + 1) * LANES]
            for k in range(Y - 1):
                a_copy(t, k).start()

        @pl.when(s > 0)
        def _():
            for j in range(4):
                part = nt_dot(
                    gate_grads, win[j * 2 * LANES : (j + 1) * 2 * LANES, :]
                ).astype(BF16)
                for n in range(2):
                    block = 2 * j + n
                    g_send[t, block % Y, block // Y] = part[:, n * LANES : (n + 1) * LANES]
            for k in range(Y - 1):
                g_copy(t, k).start()

        for block in range(2 * GATES):
            values = grads[block].astype(F32)
            grads_t[t, block] = values.T.astype(BF16)
            dbs[block : block + 1, :] += jnp.sum(values, axis=0, keepdims=True)

        @pl.when(s > 0)
        def _():
            for k in range(Y - 1):
                g_arrival(t, k).wait_recv()
            for half in range(2):
                e_send[t, half] = total(g_send, g_recv, t, half).astype(BF16).reshape(
                    Y, ROWS, LANES
                )
            e_copy(t).start()

    def db_copy(zz, p):
        return remote(
            dbs, db_in.at[z, x], db_ss.at[zz, p], db_rs.at[z, x],
            {"z": zz, "x": owner_x, "y": owner_y[p]},
        )

    def dw_copy(zz, p):
        return remote(
            dw_send.at[zz, p], dw_recv.at[z, x], dw_ss.at[zz, p], dw_rs.at[z, x],
            {"z": zz, "x": owner_x, "y": owner_y[p]},
        )

    @pl.loop(0, Z)
    def _(turn):
        zz = lax.rem(z + Z // 2 + turn, Z)
        rows = jnp.concatenate([grads_t[t, zz] for t in range(STEPS)], axis=1)
        for j in range(4):
            columns = slice(j * 2 * LANES, (j + 1) * 2 * LANES)
            part = nn_dot(rows, hmat[:, columns]).astype(BF16)
            for p in range(2):
                dw_send[zz, p, :, columns] = part[p * LANES // 2 : (p + 1) * LANES // 2, :]
        for p in range(2):
            @pl.when(is_me(zz, owner_x, owner_y[p]))
            def _():
                dw_recv[z, x] = dw_send[zz, p]
                db_in[z, x] = dbs[...]

            @pl.when(jnp.logical_not(is_me(zz, owner_x, owner_y[p])))
            def _():
                dw_copy(zz, p).start()
                db_copy(zz, p).start()

    @pl.loop(0, Z)
    def _(zz):
        for xx in range(X):
            @pl.when(jnp.logical_not(is_me(zz, xx, user_y)))
            def _():
                where = {"z": zz, "x": xx, "y": user_y}
                dw_part = dw_recv.at[zz, xx]
                db_part = db_in.at[zz, xx]
                remote(dw_part, dw_part, dw_ss.at[0, 0], dw_rs.at[zz, xx], where).wait_recv()
                remote(db_part, db_part, db_ss.at[0, 0], db_rs.at[zz, xx], where).wait_recv()

    for j in range(4):
        columns = slice(j * 2 * LANES, (j + 1) * 2 * LANES)
        weight_sum = jnp.zeros((LANES // 2, 2 * LANES), F32)
        for zz in range(Z):
            for xx in range(X):
                weight_sum = weight_sum + dw_recv[zz, xx, :, columns].astype(F32)
        dw_out[:, columns] = weight_sum
    bias_sum = jnp.zeros((1, LANES), F32)
    for zz in range(Z):
        for xx in range(X):
            bias_sum = bias_sum + db_in[zz, xx, pl.ds(z, 1), :]
    db_out[...] = jnp.where(own_half == 0, bias_sum[:, : LANES // 2], bias_sum[:, LANES // 2 :])

    for xx in range(X):
        @pl.when(jnp.logical_not(is_me(z, xx, user_y)))
        def _():
            first_hop(xx).wait_send()

    for k in range(S - 1):
        st_copy(k).wait_send()
    for step in range(Z // 2):
        ring_up(step).wait_send()
        ring_down(step).wait_send()
    for k in range(Y - 1):
        info_copy(k).wait_send()
        h0_copy(k).wait_send()
        c0_copy(k).wait_send()

    @pl.when(s == 0)
    def _():
        for k in range(Y - 1):
            obs_copy(k).wait_send()

    @pl.when(s == S - 1)
    def _():
        for k in range(Y - 1):
            cot_copy(k).wait_send()

    @pl.loop(0, STEPS)
    def _(t):
        for k in range(Y - 1):
            h_copy(t + 1, k).wait_send()

        @pl.when(s < S - 1)
        def _():
            x_copy(t).wait_send()

        @pl.when(t > 0)
        def _():
            for k in range(Y - 1):
                a_copy(t, k).wait_send()

        @pl.when(s > 0)
        def _():
            for k in range(Y - 1):
                g_copy(t, k).wait_send()
            e_copy(t).wait_send()

    @pl.loop(0, Z)
    def _(zz):
        for p in range(2):
            @pl.when(jnp.logical_not(is_me(zz, owner_x, owner_y[p])))
            def _():
                dw_copy(zz, p).wait_send()
                db_copy(zz, p).wait_send()

    hid_copy.wait()


def on_device(
    obs_features, w_input, w_recurrent, bias, stored_states, state_owner, burn_steps, valid_steps, cotangent
):
    lane = lax.broadcasted_iota(jnp.int32, (ROWS, LANES), 1)
    alive = (lane >= burn_steps[:, None]) & (lane < valid_steps[:, None])
    owned = (lane - STEPS) == state_owner[:, None]
    info = jnp.where(lane < STEPS, alive, owned).astype(F32)
    vmem = pl.BlockSpec(memory_space=pltpu.VMEM)
    hbm = pl.BlockSpec(memory_space=pl.ANY)
    dma = pltpu.SemaphoreType.DMA
    piece = (Y, ROWS, LANES)
    hidden, weights, biases = pl.pallas_call(
        kernel,
        out_shape=(
            jax.ShapeDtypeStruct((STEPS, ROWS, D), BF16),
            jax.ShapeDtypeStruct((LANES // 2, D), F32),
            jax.ShapeDtypeStruct((1, LANES // 2), F32),
        ),
        in_specs=[vmem, vmem, hbm, hbm, vmem, hbm, vmem],
        out_specs=(hbm, vmem, vmem),
        scratch_shapes=[
            pltpu.VMEM((Y, ROWS, LANES), F32),
            pltpu.VMEM((S, ROWS, 2 * D), BF16),
            pltpu.VMEM((D, LOCAL), BF16),
            pltpu.VMEM((Z, 2, LANES // 2, D), BF16),
            pltpu.VMEM((STEPS, 2, Y, *piece), BF16),
            pltpu.VMEM((STEPS + 1, 2, Y, *piece), BF16),
            pltpu.VMEM((STEPS, 2, *piece), BF16),
            pltpu.VMEM((Y, STEPS, 2, ROWS, LANES), BF16),
            pltpu.VMEM((Y, 2, ROWS, LANES), BF16),
            pltpu.VMEM((Y, 2, ROWS, LANES), BF16),
            pltpu.VMEM((STEPS + 1, 2, ALL_ROWS, LANES), F32),
            pltpu.VMEM((STEPS, GATES, 2, ALL_ROWS, LANES), F32),
            pltpu.VMEM((GATES, 2, ALL_ROWS, LANES), F32),
            pltpu.VMEM((STEPS, ALL_ROWS, LANES), F32),
            pltpu.VMEM((2 * GATES, ALL_ROWS, LANES), BF16),
            pltpu.VMEM((STEPS, 2 * GATES, LANES, ALL_ROWS), BF16),
            pltpu.VMEM((2, ALL_ROWS, LANES), F32),
            pltpu.VMEM((STEPS, Y, 2, ALL_ROWS, LANES), BF16),
            pltpu.VMEM((STEPS, Y, 2, ALL_ROWS, LANES), BF16),
            pltpu.VMEM((STEPS, Y, 2, ALL_ROWS, LANES), BF16),
            pltpu.VMEM((STEPS, Y, 2, ALL_ROWS, LANES), BF16),
            pltpu.VMEM((STEPS, 2, *piece), BF16),
            pltpu.VMEM((STEPS * ALL_ROWS, D), BF16),
            pltpu.VMEM((2 * GATES, LANES), F32),
            pltpu.VMEM((Z, X, 2 * GATES, LANES), F32),
            pltpu.VMEM((Z, 2, LANES // 2, D), BF16),
            pltpu.VMEM((Z, X, LANES // 2, D), BF16),
            pltpu.VMEM((STEPS, ROWS, D), BF16),
            dma((Y - 1,)), dma((Y - 1,)),
            dma((S - 1,)), dma((S - 1,)), dma,
            dma((X,)), dma((2,)), dma,
            dma((2, Z // 2)), dma((2, Z // 2)),
            dma((2 * GATES,)),
            dma((Y - 1,)), dma((Y - 1,)),
            dma((Y - 1,)), dma((Y - 1,)),
            dma((Y - 1,)), dma((Y - 1,)),
            dma((STEPS + 1, Y - 1)), dma((STEPS + 1, Y - 1)),
            dma((STEPS,)), dma((STEPS,)),
            dma((STEPS, Y - 1)), dma((STEPS, Y - 1)),
            dma((STEPS, Y - 1)), dma((STEPS, Y - 1)),
            dma((STEPS,)), dma((STEPS,)),
            dma((Z, 2)), dma((Z, X)),
            dma((Z, 2)), dma((Z, X)),
            dma,
        ],
        compiler_params=pltpu.CompilerParams(
            collective_id=0, has_side_effects=True, vmem_limit_bytes=56 * 1024 * 1024
        ),
        name="replay_window",
    )(
        obs_features, cotangent, w_input[0], w_recurrent[0].T, bias, stored_states[0], info
    )
    return hidden[None], weights.T[None], biases


def solution(mesh):
    axes = ("s", "z", "x", "y")
    grid = Mesh(mesh.devices.reshape(S, Z, X, Y), axes)
    dp = ("z", "x", "y")
    return jax.shard_map(
        on_device,
        mesh=grid,
        in_specs=(
            P(None, dp, None),
            P("s", None, None),
            P("s", None, dp),
            P("s", None),
            P("s", None, dp, None),
            P(dp),
            P(dp),
            P(dp),
            P(None, dp, None),
        ),
        out_specs=(P("s", None, dp, None), P("s", None, dp), P("s", dp)),
        check_vma=False,
    )
```

time: 640 us -> 255 us (0.40); the launches traced: 633 us -> 255 us
  waiting for transfers between devices: 374 us -> 0 us
  Pallas kernels: 0 us -> 248 us
  local copies, waits for them, and re-layouts: 75.1 us -> 4.45 us
  matrix products: 65.9 us -> 0 us
  starting transfers between devices: 47.9 us -> 0 us
  blocking collectives: 27.1 us -> 0 us
  other arithmetic: 18.4 us -> 1.39 us
  between operations: 16 us -> 0.65 us
  loops' own time: 8.9 us -> 0 us
    pallas_call x0 -> x1, Pallas kernels: none -> 248 us  [on_device(): pl.pallas_call(kernel, out_shape=(jax.ShapeDtypeStruct((STEPS, ROWS, D),...]
    ppermute x8 -> x0, waiting for transfers between devices: 203 us -> none  [from_behind(): return lax.ppermute(array, axis, pairs)]
    all_gather x2 -> x0, waiting for transfers between devices: 134 us -> none  [the longest x1 134 us: on_device(): w_rec = lax.all_gather(w_recurrent[0], 'dp', axis=1, tiled=True)]
    dot_general x11 -> x0, matrix products: 65.9 us -> none  [the longest x4 26.8 us: times_transposed(): lax.dot_general(operand, matrix, (((1,), (1,)), ((), ())), preferred_elem...]
    another operation x15 -> x0, local copies, waits for them, and re-layouts: 51.2 us -> none
    ppermute x8 -> x0, starting transfers between devices: 47.7 us -> none  [from_behind(): return lax.ppermute(array, axis, pairs)]
    reduce_scatter x2 -> x0, waiting for transfers between devices: 36.5 us -> none  [the longest x1 20 us: scatter_pairs(): return lax.psum_scatter(parts, chips, scatter_dimension=0, tiled=True)[0]]
    all_to_all x1 -> x0, blocking collectives: 27.1 us -> none  [on_device(): lax.all_to_all(gate_rows, 'dp', split_axis=1, concat_axis=0, tiled=True)]
  transfers between devices with their start and end apart: 12 -> 0, of which waited for: 11 -> 0; matrix products, arithmetic and copies ran while one was open for 12% -> 0% of each run, Pallas kernels for 0% -> 0%
where the time goes in v1:
time: 255 us
  Pallas kernels  248 us (97%)
  local copies, waits for them, and re-layouts  4.45 us (2%)
    pallas_call x1, Pallas kernels, on_device(): pl.pallas_call(kernel, out_shape=(jax.ShapeDtypeStruct((STEPS, ROWS, D),...  248 us

profile of v1, /device:TPU:24, one launch (start us, length us, event | category | flops | bytes accessed | tf_op | source)
XLA Modules:
  0.0 254.8 jit_solution(16452013726148878198)
XLA Ops:
  0.7 1.4 fusion.2.info_ref
  2.0 248.3 %replay_window.1 = (bf16[4,32,1024]{2,1,0:T(8,128)(2,1)}, f32[64,1024]{1,0:T(8,128)}, f32[1,64]{1,0:T(1,128)}) custom-call(bf16[4,32,1024]{2,1,0:T(8,128)(2,1)} %obs_ref.1, bf16[4,32,1024]{2,1,0:T(8,128)(2,1)} %cot_ref.1, bf16[1024,4096]{1,0:T(8,128)(2,1)} %bitcast.9, bf16[64,1024]{1,0:T(8,128)(2,1)} %bitcast.13, f32[1,4096]{1,0:T(1,128)} %bias_ref.1, ...), custom_call_target="tpu_custom_call" | custom-call | tf_op jit(solution)/shard_map/replay_window/pallas_call | solution.py:628
  250.4 1.7 copy.15
  252.0 1.7 copy.16
  253.7 1.1 copy.17
  (2 shorter events, 0.0 us)

commit v2 on v1

--- a/solution.py
+++ b/solution.py
@@ -43,15 +43,17 @@
 
 
 def kernel(
-    obs_ref, cot_ref, win_hbm, wrt_hbm, bias_ref, st_hbm, info_ref,
+    obs_hbm, cot_hbm, win_hbm, wrt_hbm, bias_ref, st_hbm, owner_ref, burn_ref, valid_ref,
     hid_out, dw_out, db_out,
-    info, st, win, wrt, xb, hb, eb, cot_st, c_st, c_in, cells, gates, acc, live,
-    grads, grads_t, carry, a_send, a_recv, g_send, g_recv, e_send, hmat, dbs, db_in,
-    dw_send, dw_recv, hid_st,
-    info_ss, info_rs, st_ss, st_rs, st_ls, wa_ss, wa_rs, wa_ls, ring_ss, ring_rs, win_ls,
-    obs_ss, obs_rs, cot_ss, cot_rs, c_ss, c_rs, h_ss, h_rs, x_ss, x_rs,
-    a_ss, a_rs, g_ss, g_rs, e_ss, e_rs, dw_ss, dw_rs, db_ss, db_rs, hid_ls,
+    obs_st, cot_in, info, st, wts, wrt, wint, act, hb_pair, eb, cot_st, c_st, c_in, cells, gates, acc, live,
+    grads, grads_t, grads_pair, carry, a_send, a_recv, g_send, g_recv, e_send, hmat, hmat_pair,
+    dw_acc, dw_send, dw_recv, db_send, db_recv, dw2_send, dw2_recv, db2_send, db2_recv, hid_st,
+    in_ls, info_ss, info_rs, st_ss, st_rs, st_ls, wa_ss, wa_rs, wa_ls, ring_ss, ring_rs, win_ls,
+    obs_ss, obs_rs, cot_ss, cot_rs, c_ss, c_rs, h_ss, h_rs, x_ss, x_rs, hz_ss, hz_rs, gz_ss, gz_rs,
+    a_ss, a_rs, g_ss, g_rs, e_ss, e_rs, dw_ss, dw_rs, db_ss, db_rs,
+    dw2_ss, dw2_rs, db2_ss, db2_rs, hid_ls,
 ):
+    xb, hb = act.at[0], act.at[1]
     s = lax.axis_index("s")
     z = lax.axis_index("z")
     x = lax.axis_index("x")
@@ -61,6 +63,13 @@
     up_s = [lax.rem(s + k, S) for k in range(1, S)]
     down_s = [lax.rem(s + S - k, S) for k in range(1, S)]
     z_up, z_down = lax.rem(z + 1, Z), lax.rem(z + Z - 1, Z)
+    z_half = lax.rem(z, 2)
+    z_other = 1 - z_half
+    z_pair = z + 1 - 2 * z_half
+    quad = z // 2
+    QUADS = Z // 2
+    far = [lax.rem(quad + k, QUADS) for k in (2, 1, 3)]
+    near = [lax.rem(quad + QUADS - k, QUADS) for k in (2, 1, 3)]
     own_half = lax.rem(y, 2)
     user_y = 2 * x + y // 2
     owner_x = y // 2
@@ -80,20 +89,31 @@
         greet({"s": down_s[k]})
     greet({"z": z_up})
     greet({"z": z_down})
+    for k in range(QUADS - 1):
+        greet({"z": 2 * near[k] + z_half})
     for p in range(2):
         @pl.when(jnp.logical_not(is_me(z, owner_x, owner_y[p])))
         def _():
             greet({"x": owner_x, "y": owner_y[p]})
 
-    @pl.loop(0, Z)
-    def _(zz):
-        for xx in range(X):
-            @pl.when(jnp.logical_not(is_me(zz, xx, user_y)))
-            def _():
-                greet({"z": zz, "x": xx, "y": user_y})
+    for xx in range(X):
+        @pl.when(jnp.logical_not(is_me(z, xx, user_y)))
+        def _():
+            greet({"x": xx, "y": user_y})
 
     mine = is_me(z, owner_x, owner_y[0]) | is_me(z, owner_x, owner_y[1])
-    base = (Y - 1) + (S - 1) + 2 + X + Z * 2
+    base = (Y - 1) + (S - 1) + 2 + (QUADS - 1) + X + 2
+    obs_copy_in = pltpu.make_async_copy(obs_hbm, obs_st, in_ls.at[0])
+    cot_copy_in = pltpu.make_async_copy(cot_hbm, cot_in, in_ls.at[1])
+
+    @pl.when(s == 0)
+    def _():
+        obs_copy_in.start()
+
+    @pl.when(s == S - 1)
+    def _():
+        cot_copy_in.start()
+
     pl.semaphore_wait(barrier, jnp.where(mine, base - 2, base))
 
     def first_hop(xx):
@@ -130,7 +150,7 @@
         block = gate * 2 + half
         return pltpu.make_async_copy(
             win_hbm.at[:, pl.ds(first, LANES)],
-            win.at[:, pl.ds(block * LANES, LANES)],
+            wts.at[0, block],
             win_ls.at[block],
         )
 
@@ -138,7 +158,14 @@
         for half in range(2):
             win_copy(gate, half).start()
 
-    info[y] = info_ref[...]
+    def column(row_ref):
+        row = jnp.broadcast_to(row_ref[...].astype(F32), (ROWS, ROWS))
+        down = lax.broadcasted_iota(jnp.int32, (ROWS, ROWS), 0)
+        across = lax.broadcasted_iota(jnp.int32, (ROWS, ROWS), 1)
+        return jnp.sum(jnp.where(down == across, row, 0.0), axis=1, keepdims=True)
+
+    lane = lax.broadcasted_iota(jnp.int32, (ROWS, LANES), 1)
+    info[y] = jnp.where(lane == 0, column(burn_ref), column(valid_ref))
 
     def info_copy(k):
         return remote(info.at[y], info.at[y], info_ss.at[k], info_rs.at[k], {"y": up_y[k]})
@@ -162,11 +189,12 @@
 
     @pl.when(s == 0)
     def _():
+        obs_copy_in.wait()
         for t in range(STEPS):
             for half in range(2):
                 for yy in range(Y):
                     first = (half * Y + yy) * LANES
-                    xb[t, half, yy, y] = obs_ref[t, :, first : first + LANES]
+                    xb[t, half, yy, y] = obs_st[t, :, first : first + LANES]
         for k in range(Y - 1):
             obs_copy(k).start()
 
@@ -181,41 +209,47 @@
 
     @pl.when(s == S - 1)
     def _():
+        cot_copy_in.wait()
         for t in range(STEPS):
             for half in range(2):
                 for yy in range(Y):
                     first = (half * Y + yy) * LANES
-                    cot_st[yy, t, half] = cot_ref[t, :, first : first + LANES]
+                    cot_st[yy, t, half] = cot_in[t, :, first : first + LANES]
         for t in range(STEPS):
             for half in range(2):
                 eb[t, half, y] = cot_st[y, t, half]
         for k in range(Y - 1):
             cot_copy(k).start()
 
-    def ring_up(step):
-        part = wrt.at[lax.rem(z + Z - step, Z)]
-        if step == Z // 2 - 1:
-            part = part.at[0]
-        return remote(part, part, ring_ss.at[0, step], ring_rs.at[0, step], {"z": z_up})
-
-    def ring_down(step):
-        part = wrt.at[lax.rem(z + step, Z)]
-        if step == Z // 2 - 1:
-            part = part.at[1]
-        return remote(part, part, ring_ss.at[1, step], ring_rs.at[1, step], {"z": z_down})
-
-    def ring_wait(step):
-        from_down = wrt.at[lax.rem(z + Z - 1 - step, Z)]
-        from_up = wrt.at[lax.rem(z + 1 + step, Z)]
-        if step == Z // 2 - 1:
-            from_down = from_down.at[0]
-            from_up = from_up.at[1]
-        remote(
-            from_down, from_down, ring_ss.at[0, step], ring_rs.at[0, step], {"z": z_up}
-        ).wait_recv()
-        remote(
-            from_up, from_up, ring_ss.at[1, step], ring_rs.at[1, step], {"z": z_down}
-        ).wait_recv()
+    def ring(way, step, p):
+        part = wrt.at[lax.rem(z + Z - step, Z) if way == 0 else lax.rem(z + step, Z), p]
+        return remote(
+            part, part, ring_ss.at[way, step, p], ring_rs.at[way, step, p],
+            {"z": z_up if way == 0 else z_down},
+        )
+
+    def ring_arrival(way, step, p):
+        part = wrt.at[lax.rem(z + Z - 1 - step, Z) if way == 0 else lax.rem(z + 1 + step, Z), p]
+        return remote(
+            part, part, ring_ss.at[way, step, p], ring_rs.at[way, step, p],
+            {"z": z_up if way == 0 else z_down},
+        )
+
+    def ring_has(way, step, p):
+        return step < Z // 2 - 1 or p == way
+
+    def ring_turn(step):
+        for p in range(2):
+            for way in range(2):
+                if ring_has(way, step - 1, p):
+                    ring_arrival(way, step - 1, p).wait_recv()
+                if step < Z // 2 and ring_has(way, step, p):
+                    ring(way, step, p).start()
+
+    def turn_block(plane):
+        block = wrt[plane].reshape(LANES, D)
+        for n in range(2 * Y):
+            wts[1, plane, n * LANES : (n + 1) * LANES, :] = block[:, n * LANES : (n + 1) * LANES].T
 
     for p in range(2):
         @pl.when(is_me(z, owner_x, owner_y[p]))
@@ -229,22 +263,26 @@
                 part, part, wa_ss.at[0], wa_rs.at[p], {"x": owner_x, "y": owner_y[p]}
             ).wait_recv()
 
-    ring_up(0).start()
-    ring_down(0).start()
+        for way in range(2):
+            ring(way, 0, p).start()
 
     st_own.wait()
     for k in range(S - 1):
         st_arrival(k).wait_recv()
-    marks = info[y]
-    chosen = jnp.zeros((ROWS, 2 * D), F32)
-    for owner in range(S):
-        here = marks[:, STEPS + owner : STEPS + owner + 1] > 0.5
-        chosen = chosen + jnp.where(here, st[owner].astype(F32), 0.0)
+    owners = jnp.broadcast_to(column(owner_ref), (ROWS, LANES))
+
+    def chosen(first):
+        value = jnp.zeros((ROWS, LANES), F32)
+        for owner in range(S):
+            entry = st[owner, :, first : first + LANES].astype(F32)
+            value = value + jnp.where(owners == float(owner), entry, 0.0)
+        return value.astype(BF16)
+
     for half in range(2):
         for yy in range(Y):
             first = (half * Y + yy) * LANES
-            hb[0, half, yy, y] = chosen[:, first : first + LANES].astype(BF16)
-            c_st[yy, half] = chosen[:, D + first : D + first + LANES].astype(BF16)
+            hb[0, half, yy, y] = chosen(first)
+            c_st[yy, half] = chosen(D + first)
     c_in[y] = c_st[y]
 
     def h0_copy(k):
@@ -266,31 +304,44 @@
         h0_copy(k).start()
         c0_copy(k).start()
 
-    ring_wait(0)
-    ring_up(1).start()
-    ring_down(1).start()
-
+    turn_block(z)
+    ring_turn(1)
+    turn_block(z_up)
+    turn_block(z_down)
     for k in range(Y - 1):
         info_arrival(k).wait_recv()
         c0_arrival(k).wait_recv()
     marks_all = info[...].reshape(ALL_ROWS, LANES)
     for t in range(STEPS):
-        live[t] = jnp.broadcast_to(marks_all[:, t : t + 1], (ALL_ROWS, LANES))
+        alive_now = (marks_all[:, 0:1] <= float(t)) & (marks_all[:, 1:2] > float(t))
+        live[t] = jnp.broadcast_to(jnp.where(alive_now, 1.0, 0.0), (ALL_ROWS, LANES))
     for half in range(2):
         cells[0, half] = c_in[:, half].reshape(ALL_ROWS, LANES).astype(F32)
+
+    ring_turn(2)
+    turn_block(lax.rem(z + 2, Z))
+    turn_block(lax.rem(z + Z - 2, Z))
     for gate in range(GATES):
         for half in range(2):
             win_copy(gate, half).wait()
 
-    ring_wait(1)
-    ring_up(2).start()
-    ring_down(2).start()
+    ring_turn(3)
+    turn_block(lax.rem(z + 3, Z))
+    turn_block(lax.rem(z + Z - 3, Z))
 
     @pl.when(s == 0)
     def _():
         for k in range(Y - 1):
             obs_arrival(k).wait_recv()
 
+    @pl.when(s > 0)
+    def _():
+        @pl.loop(0, 2 * GATES)
+        def _(block):
+            for n in range(2 * Y):
+                piece = wts[0, block, n * LANES : (n + 1) * LANES, :]
+                wint[block, :, n * LANES : (n + 1) * LANES] = piece.T
+
     @pl.when(s == S - 1)
     def _():
         for k in range(Y - 1):
@@ -299,15 +350,20 @@
     for k in range(Y - 1):
         h0_arrival(k).wait_recv()
 
-    ring_wait(2)
-    ring_up(3).start()
-    ring_down(3).start()
-    ring_wait(3)
-
-    def whole(ref, t):
+    def hz_copy(t):
+        return remote(hb.at[t], hb_pair.at[t], hz_ss.at[t], hz_rs.at[t], {"z": z_pair})
+
+    def hz_arrival(t):
+        return remote(hb_pair.at[t], hb_pair.at[t], hz_ss.at[t], hz_rs.at[t], {"z": z_pair})
+
+    ring_turn(4)
+    turn_block(lax.rem(z + Z // 2, Z))
+    hz_copy(0).start()
+
+    def whole(ref, *at):
         return jnp.concatenate(
             [
-                ref[t, half, yy].reshape(ALL_ROWS, LANES)
+                ref[(*at, half, yy)].reshape(ALL_ROWS, LANES)
                 for half in range(2)
                 for yy in range(Y)
             ],
@@ -336,22 +392,31 @@
         def _():
             x_copy(t).start()
 
-    def project(t):
-        inputs = whole(xb, t)
+        @pl.when(t < STEPS - 1)
+        def _():
+            hz_copy(t + 1).start()
+
+    def product(kind, inputs, gate):
+        weights = jnp.concatenate([wts[kind, 2 * gate], wts[kind, 2 * gate + 1]], axis=1)
+        return nn_dot(inputs, weights)
+
+    def first_product(kind, t):
+        inputs = whole(act, kind, t)
         for gate in range(GATES):
-            columns = slice(gate * 2 * LANES, (gate + 1) * 2 * LANES)
-            part = nn_dot(inputs, win[:, columns])
+            part = product(kind, inputs, gate)
             for half in range(2):
                 first = pl.multiple_of(gate * D + half * Y * LANES + y * LANES, LANES)
                 acc[gate, half] = (
                     part[:, half * LANES : (half + 1) * LANES] + bias_ref[:, pl.ds(first, LANES)]
                 )
 
+    last_kind = jnp.where(s == 0, 1, 0)
+
     @pl.loop(0, STEPS)
     def _(t):
         @pl.when(s == 0)
         def _():
-            project(t)
+            first_product(0, t)
 
         @pl.when(t > 0)
         def _():
@@ -359,13 +424,12 @@
 
         @pl.when(s > 0)
         def _():
+            first_product(1, t)
             x_arrival(t).wait_recv()
-            project(t)
-
-        before = whole(hb, t)
+
+        inputs = whole(act, last_kind, t)
         for gate in range(GATES):
-            rows = wrt[2 * gate : 2 * gate + 2].reshape(2 * LANES, D)
-            part = nt_dot(before, rows)
+            part = product(last_kind, inputs, gate)
             for half in range(2):
                 pre = acc[gate, half] + part[:, half * LANES : (half + 1) * LANES]
                 gates[t, gate, half] = jnp.tanh(pre) if gate == 2 else sigmoid(pre)
@@ -380,18 +444,30 @@
             h_copy(t + 1, k).start()
 
     pass_up(STEPS - 1)
-    for t in range(STEPS):
-        for half in range(2):
-            for yy in range(Y):
-                first = (half * Y + yy) * LANES
-                hid_st[t, :, first : first + LANES] = hb[t + 1, half, yy, y]
     hid_copy = pltpu.make_async_copy(hid_st, hid_out, hid_ls)
-    hid_copy.start()
-    for t in range(STEPS):
-        hmat[t * ALL_ROWS : (t + 1) * ALL_ROWS, :] = whole(hb, t)
+
+    def keep_hidden():
+        for t in range(STEPS):
+            for half in range(2):
+                for yy in range(Y):
+                    first = (half * Y + yy) * LANES
+                    hid_st[t, :, first : first + LANES] = hb[t + 1, half, yy, y]
+        hid_copy.start()
+        for t in range(STEPS):
+            hz_arrival(t).wait_recv()
+            hmat[t * ALL_ROWS : (t + 1) * ALL_ROWS, :] = whole(hb, t)
+            hmat_pair[t * ALL_ROWS : (t + 1) * ALL_ROWS, :] = whole(hb_pair, t)
 
     carry[...] = jnp.zeros_like(carry)
-    dbs[...] = jnp.zeros_like(dbs)
+
+    def gz_copy(t):
+        return remote(
+            grads_t.at[t, z_other], grads_pair.at[t], gz_ss.at[t], gz_rs.at[t], {"z": z_pair}
+        )
+
+    def gz_arrival(t):
+        part = grads_pair.at[t]
+        return remote(part, part, gz_ss.at[t], gz_rs.at[t], {"z": z_pair})
 
     def a_copy(t, k):
         return remote(
@@ -478,8 +554,9 @@
         @pl.when(s > 0)
         def _():
             for j in range(4):
-                part = nt_dot(
-                    gate_grads, win[j * 2 * LANES : (j + 1) * 2 * LANES, :]
+                columns = slice(j * 2 * LANES, (j + 1) * 2 * LANES)
+                part = nn_dot(
+                    gate_grads, wint[:, :, columns].reshape(LOCAL, 2 * LANES)
                 ).astype(BF16)
                 for n in range(2):
                     block = 2 * j + n
@@ -487,10 +564,14 @@
             for k in range(Y - 1):
                 g_copy(t, k).start()
 
-        for block in range(2 * GATES):
-            values = grads[block].astype(F32)
-            grads_t[t, block] = values.T.astype(BF16)
-            dbs[block : block + 1, :] += jnp.sum(values, axis=0, keepdims=True)
+        for gate in range(GATES):
+            for half in range(2):
+                grads_t[t, half, gate] = grads[2 * gate + half].T
+        gz_copy(t).start()
+
+        @pl.when(back == 0)
+        def _():
+            keep_hidden()
 
         @pl.when(s > 0)
         def _():
@@ -502,60 +583,103 @@
                 )
             e_copy(t).start()
 
-    def db_copy(zz, p):
-        return remote(
-            dbs, db_in.at[z, x], db_ss.at[zz, p], db_rs.at[z, x],
-            {"z": zz, "x": owner_x, "y": owner_y[p]},
-        )
-
-    def dw_copy(zz, p):
-        return remote(
-            dw_send.at[zz, p], dw_recv.at[z, x], dw_ss.at[zz, p], dw_rs.at[z, x],
-            {"z": zz, "x": owner_x, "y": owner_y[p]},
-        )
-
-    @pl.loop(0, Z)
-    def _(turn):
-        zz = lax.rem(z + Z // 2 + turn, Z)
-        rows = jnp.concatenate([grads_t[t, zz] for t in range(STEPS)], axis=1)
+    def dw_copy(k):
+        return remote(
+            dw_send.at[far[k]], dw_recv.at[quad], dw_ss.at[k], dw_rs.at[k],
+            {"z": 2 * far[k] + z_half},
+        )
+
+    def dw_arrival(k):
+        part = dw_recv.at[near[k]]
+        return remote(part, part, dw_ss.at[k], dw_rs.at[k], {"z": 2 * far[k] + z_half})
+
+    def db_copy(k):
+        return remote(
+            db_send.at[far[k]], db_recv.at[quad], db_ss.at[k], db_rs.at[k],
+            {"z": 2 * far[k] + z_half},
+        )
+
+    def db_arrival(k):
+        part = db_recv.at[near[k]]
+        return remote(part, part, db_ss.at[k], db_rs.at[k], {"z": 2 * far[k] + z_half})
+
+    for t in range(1, STEPS):
+        gz_arrival(t).wait_recv()
+
+    @pl.loop(0, GATES)
+    def _(gate):
+        rows = jnp.concatenate([grads_t[t, z_half, gate] for t in range(STEPS)], axis=1)
+        rows_pair = jnp.concatenate([grads_pair[t, gate] for t in range(1, STEPS)], axis=1)
         for j in range(4):
             columns = slice(j * 2 * LANES, (j + 1) * 2 * LANES)
-            part = nn_dot(rows, hmat[:, columns]).astype(BF16)
-            for p in range(2):
-                dw_send[zz, p, :, columns] = part[p * LANES // 2 : (p + 1) * LANES // 2, :]
-        for p in range(2):
-            @pl.when(is_me(zz, owner_x, owner_y[p]))
-            def _():
-                dw_recv[z, x] = dw_send[zz, p]
-                db_in[z, x] = dbs[...]
-
-            @pl.when(jnp.logical_not(is_me(zz, owner_x, owner_y[p])))
-            def _():
-                dw_copy(zz, p).start()
-                db_copy(zz, p).start()
-
-    @pl.loop(0, Z)
-    def _(zz):
-        for xx in range(X):
-            @pl.when(jnp.logical_not(is_me(zz, xx, user_y)))
-            def _():
-                where = {"z": zz, "x": xx, "y": user_y}
-                dw_part = dw_recv.at[zz, xx]
-                db_part = db_in.at[zz, xx]
-                remote(dw_part, dw_part, dw_ss.at[0, 0], dw_rs.at[zz, xx], where).wait_recv()
-                remote(db_part, db_part, db_ss.at[0, 0], db_rs.at[zz, xx], where).wait_recv()
-
-    for j in range(4):
-        columns = slice(j * 2 * LANES, (j + 1) * 2 * LANES)
-        weight_sum = jnp.zeros((LANES // 2, 2 * LANES), F32)
-        for zz in range(Z):
-            for xx in range(X):
-                weight_sum = weight_sum + dw_recv[zz, xx, :, columns].astype(F32)
-        dw_out[:, columns] = weight_sum
-    bias_sum = jnp.zeros((1, LANES), F32)
-    for zz in range(Z):
-        for xx in range(X):
-            bias_sum = bias_sum + db_in[zz, xx, pl.ds(z, 1), :]
+            dw_acc[gate, :, columns] = nn_dot(rows, hmat[:, columns]) + nn_dot(
+                rows_pair, hmat_pair[ALL_ROWS:, columns]
+            )
+        db_send[gate] = nt_dot(jnp.ones((8, STEPS * ALL_ROWS), BF16), rows) + nt_dot(
+            jnp.ones((8, (STEPS - 1) * ALL_ROWS), BF16), rows_pair
+        )
+
+    gz_arrival(0).wait_recv()
+    for k in range(QUADS):
+        gate = far[k] if k < QUADS - 1 else quad
+        rows_pair = grads_pair[0, gate]
+        db_send[gate] = db_send[gate] + nt_dot(jnp.ones((8, ALL_ROWS), BF16), rows_pair)
+        for j in range(4):
+            columns = slice(j * 2 * LANES, (j + 1) * 2 * LANES)
+            part = dw_acc[gate, :, columns] + nn_dot(rows_pair, hmat_pair[:ALL_ROWS, columns])
+            if k < QUADS - 1:
+                dw_send[gate, :, columns] = part.astype(BF16)
+            else:
+                dw_acc[gate, :, columns] = part
+        if k < QUADS - 1:
+            db_copy(k).start()
+            dw_copy(k).start()
+
+    def dw2_copy(p):
+        return remote(
+            dw2_send.at[p], dw2_recv.at[x], dw2_ss.at[p], dw2_rs.at[x],
+            {"x": owner_x, "y": owner_y[p]},
+        )
+
+    def db2_copy(p):
+        return remote(
+            db2_send, db2_recv.at[x], db2_ss.at[p], db2_rs.at[x],
+            {"x": owner_x, "y": owner_y[p]},
+        )
+
+    for k in range(QUADS - 1):
+        db_arrival(k).wait_recv()
+    db2_send[...] = db_send[quad] + db_recv[near[0]] + db_recv[near[1]] + db_recv[near[2]]
+    for k in range(QUADS - 1):
+        dw_arrival(k).wait_recv()
+    for p in range(2):
+        rows = slice(p * LANES // 2, (p + 1) * LANES // 2)
+        value = dw_acc[quad, rows, :]
+        for k in range(QUADS - 1):
+            value = value + dw_recv[near[k], rows, :].astype(F32)
+        dw2_send[p] = value.astype(BF16)
+
+        @pl.when(is_me(z, owner_x, owner_y[p]))
+        def _():
+            dw2_recv[x] = dw2_send[p]
+            db2_recv[x] = db2_send[...]
+
+        @pl.when(jnp.logical_not(is_me(z, owner_x, owner_y[p])))
+        def _():
+            db2_copy(p).start()
+            dw2_copy(p).start()
+
+    for xx in range(X):
+        @pl.when(jnp.logical_not(is_me(z, xx, user_y)))
+        def _():
+            where = {"x": xx, "y": user_y}
+            dw_part = dw2_recv.at[xx]
+            db_part = db2_recv.at[xx]
+            remote(db_part, db_part, db2_ss.at[0], db2_rs.at[xx], where).wait_recv()
+            remote(dw_part, dw_part, dw2_ss.at[0], dw2_rs.at[xx], where).wait_recv()
+
+    dw_out[...] = dw2_recv[0].astype(F32) + dw2_recv[1].astype(F32)
+    bias_sum = db2_recv[0, 0:1, :] + db2_recv[1, 0:1, :]
     db_out[...] = jnp.where(own_half == 0, bias_sum[:, : LANES // 2], bias_sum[:, LANES // 2 :])
 
     for xx in range(X):
@@ -566,8 +690,10 @@
     for k in range(S - 1):
         st_copy(k).wait_send()
     for step in range(Z // 2):
-        ring_up(step).wait_send()
-        ring_down(step).wait_send()
+        for p in range(2):
+            for way in range(2):
+                if ring_has(way, step, p):
+                    ring(way, step, p).wait_send()
     for k in range(Y - 1):
         info_copy(k).wait_send()
         h0_copy(k).wait_send()
@@ -592,6 +718,9 @@
         def _():
             x_copy(t).wait_send()
 
+        hz_copy(t).wait_send()
+        gz_copy(t).wait_send()
+
         @pl.when(t > 0)
         def _():
             for k in range(Y - 1):
@@ -603,13 +732,14 @@
                 g_copy(t, k).wait_send()
             e_copy(t).wait_send()
 
-    @pl.loop(0, Z)
-    def _(zz):
-        for p in range(2):
-            @pl.when(jnp.logical_not(is_me(zz, owner_x, owner_y[p])))
-            def _():
-                dw_copy(zz, p).wait_send()
-                db_copy(zz, p).wait_send()
+    for k in range(QUADS - 1):
+        dw_copy(k).wait_send()
+        db_copy(k).wait_send()
+    for p in range(2):
+        @pl.when(jnp.logical_not(is_me(z, owner_x, owner_y[p])))
+        def _():
+            dw2_copy(p).wait_send()
+            db2_copy(p).wait_send()
 
     hid_copy.wait()
 
@@ -617,10 +747,6 @@
 def on_device(
     obs_features, w_input, w_recurrent, bias, stored_states, state_owner, burn_steps, valid_steps, cotangent
 ):
-    lane = lax.broadcasted_iota(jnp.int32, (ROWS, LANES), 1)
-    alive = (lane >= burn_steps[:, None]) & (lane < valid_steps[:, None])
-    owned = (lane - STEPS) == state_owner[:, None]
-    info = jnp.where(lane < STEPS, alive, owned).astype(F32)
     vmem = pl.BlockSpec(memory_space=pltpu.VMEM)
     hbm = pl.BlockSpec(memory_space=pl.ANY)
     dma = pltpu.SemaphoreType.DMA
@@ -632,15 +758,18 @@
             jax.ShapeDtypeStruct((LANES // 2, D), F32),
             jax.ShapeDtypeStruct((1, LANES // 2), F32),
         ),
-        in_specs=[vmem, vmem, hbm, hbm, vmem, hbm, vmem],
+        in_specs=[hbm, hbm, hbm, hbm, vmem, hbm, vmem, vmem, vmem],
         out_specs=(hbm, vmem, vmem),
         scratch_shapes=[
+            pltpu.VMEM((STEPS, ROWS, D), BF16),
+            pltpu.VMEM((STEPS, ROWS, D), BF16),
             pltpu.VMEM((Y, ROWS, LANES), F32),
             pltpu.VMEM((S, ROWS, 2 * D), BF16),
-            pltpu.VMEM((D, LOCAL), BF16),
+            pltpu.VMEM((2, Z, D, LANES), BF16),
             pltpu.VMEM((Z, 2, LANES // 2, D), BF16),
+            pltpu.VMEM((2 * GATES, LANES, D), BF16),
+            pltpu.VMEM((2, STEPS + 1, 2, Y, *piece), BF16),
             pltpu.VMEM((STEPS, 2, Y, *piece), BF16),
-            pltpu.VMEM((STEPS + 1, 2, Y, *piece), BF16),
             pltpu.VMEM((STEPS, 2, *piece), BF16),
             pltpu.VMEM((Y, STEPS, 2, ROWS, LANES), BF16),
             pltpu.VMEM((Y, 2, ROWS, LANES), BF16),
@@ -650,7 +779,8 @@
             pltpu.VMEM((GATES, 2, ALL_ROWS, LANES), F32),
             pltpu.VMEM((STEPS, ALL_ROWS, LANES), F32),
             pltpu.VMEM((2 * GATES, ALL_ROWS, LANES), BF16),
-            pltpu.VMEM((STEPS, 2 * GATES, LANES, ALL_ROWS), BF16),
+            pltpu.VMEM((STEPS, 2, GATES, LANES, ALL_ROWS), BF16),
+            pltpu.VMEM((STEPS, GATES, LANES, ALL_ROWS), BF16),
             pltpu.VMEM((2, ALL_ROWS, LANES), F32),
             pltpu.VMEM((STEPS, Y, 2, ALL_ROWS, LANES), BF16),
             pltpu.VMEM((STEPS, Y, 2, ALL_ROWS, LANES), BF16),
@@ -658,26 +788,37 @@
             pltpu.VMEM((STEPS, Y, 2, ALL_ROWS, LANES), BF16),
             pltpu.VMEM((STEPS, 2, *piece), BF16),
             pltpu.VMEM((STEPS * ALL_ROWS, D), BF16),
-            pltpu.VMEM((2 * GATES, LANES), F32),
-            pltpu.VMEM((Z, X, 2 * GATES, LANES), F32),
-            pltpu.VMEM((Z, 2, LANES // 2, D), BF16),
-            pltpu.VMEM((Z, X, LANES // 2, D), BF16),
+            pltpu.VMEM((STEPS * ALL_ROWS, D), BF16),
+            pltpu.VMEM((GATES, LANES, D), F32),
+            pltpu.VMEM((GATES, LANES, D), BF16),
+            pltpu.VMEM((GATES, LANES, D), BF16),
+            pltpu.VMEM((GATES, 8, LANES), F32),
+            pltpu.VMEM((GATES, 8, LANES), F32),
+            pltpu.VMEM((2, LANES // 2, D), BF16),
+            pltpu.VMEM((X, LANES // 2, D), BF16),
+            pltpu.VMEM((8, LANES), F32),
+            pltpu.VMEM((X, 8, LANES), F32),
             pltpu.VMEM((STEPS, ROWS, D), BF16),
+            dma((2,)),
             dma((Y - 1,)), dma((Y - 1,)),
             dma((S - 1,)), dma((S - 1,)), dma,
             dma((X,)), dma((2,)), dma,
-            dma((2, Z // 2)), dma((2, Z // 2)),
+            dma((2, Z // 2, 2)), dma((2, Z // 2, 2)),
             dma((2 * GATES,)),
             dma((Y - 1,)), dma((Y - 1,)),
             dma((Y - 1,)), dma((Y - 1,)),
             dma((Y - 1,)), dma((Y - 1,)),
             dma((STEPS + 1, Y - 1)), dma((STEPS + 1, Y - 1)),
             dma((STEPS,)), dma((STEPS,)),
+            dma((STEPS,)), dma((STEPS,)),
+            dma((STEPS,)), dma((STEPS,)),
             dma((STEPS, Y - 1)), dma((STEPS, Y - 1)),
             dma((STEPS, Y - 1)), dma((STEPS, Y - 1)),
             dma((STEPS,)), dma((STEPS,)),
-            dma((Z, 2)), dma((Z, X)),
-            dma((Z, 2)), dma((Z, X)),
+            dma((3,)), dma((3,)),
+            dma((3,)), dma((3,)),
+            dma((2,)), dma((X,)),
+            dma((2,)), dma((X,)),
             dma,
         ],
         compiler_params=pltpu.CompilerParams(
@@ -685,7 +826,8 @@
         ),
         name="replay_window",
     )(
-        obs_features, cotangent, w_input[0], w_recurrent[0].T, bias, stored_states[0], info
+        obs_features, cotangent, w_input[0], w_recurrent[0].T, bias, stored_states[0],
+        state_owner[None], burn_steps[None], valid_steps[None],
     )
     return hidden[None], weights.T[None], biases
 

time: 255 us -> 180 us (0.71)
  Pallas kernels: 248 us -> 173 us
    pallas_call x1, Pallas kernels: 248 us -> 173 us  [on_device(): pl.pallas_call(kernel, out_shape=(jax.ShapeDtypeStruct((STEPS, ROWS, D),...]
where the time goes in v2:
time: 180 us; the launch traced here: 178 us
  Pallas kernels  173 us (96%)
  local copies, waits for them, and re-layouts  4.45 us (2%)
    pallas_call x1, Pallas kernels, on_device(): pl.pallas_call(kernel, out_shape=(jax.ShapeDtypeStruct((STEPS, ROWS, D),...  173 us
    unnamed x3, local copies, waits for them, and re-layouts  4.45 us

profile of v2, /device:TPU:24, one launch (start us, length us, event | category | flops | bytes accessed | tf_op | source)
XLA Modules:
  0.0 178.5 jit_solution(16021515430779039945)
XLA Ops:
  0.6 173.4 %replay_window.1 = (bf16[4,32,1024]{2,1,0:T(8,128)(2,1)}, f32[64,1024]{1,0:T(8,128)}, f32[1,64]{1,0:T(1,128)}) custom-call(bf16[4,32,1024]{2,1,0:T(8,128)(2,1)} %obs_hbm.1, bf16[4,32,1024]{2,1,0:T(8,128)(2,1)} %cot_hbm.1, bf16[1024,4096]{1,0:T(8,128)(2,1)} %bitcast.12, bf16[64,1024]{1,0:T(8,128)(2,1)} %bitcast.16, f32[1,4096]{1,0:T(1,128)} %bias_ref.1, ...), custom_call_target="tpu_custom_call" | custom-call | tf_op jit(solution)/shard_map/replay_window/pallas_call | solution.py:754
  174.0 1.7 copy.15
  175.7 1.7 copy.16
  177.4 1.1 copy.17

commit v3 on v2

--- a/solution.py
+++ b/solution.py
@@ -11,6 +11,7 @@
 ROWS = 32
 D = 1024
 LANES = 128
+ORDER = (0, 2, 1, 3)
 GATES = 4
 ALL_ROWS = Y * ROWS
 LOCAL = GATES * 2 * LANES
@@ -47,11 +48,11 @@
     hid_out, dw_out, db_out,
     obs_st, cot_in, info, st, wts, wrt, wint, act, hb_pair, eb, cot_st, c_st, c_in, cells, gates, acc, live,
     grads, grads_t, grads_pair, carry, a_send, a_recv, g_send, g_recv, e_send, hmat, hmat_pair,
-    dw_acc, dw_send, dw_recv, db_send, db_recv, dw2_send, dw2_recv, db2_send, db2_recv, hid_st,
+    dw_acc, dw_send, dw_recv, db_send, db_recv, dw2_send, dw2_recv, db2_send, db2_recv,
     in_ls, info_ss, info_rs, st_ss, st_rs, st_ls, wa_ss, wa_rs, wa_ls, ring_ss, ring_rs, win_ls,
     obs_ss, obs_rs, cot_ss, cot_rs, c_ss, c_rs, h_ss, h_rs, x_ss, x_rs, hz_ss, hz_rs, gz_ss, gz_rs,
     a_ss, a_rs, g_ss, g_rs, e_ss, e_rs, dw_ss, dw_rs, db_ss, db_rs,
-    dw2_ss, dw2_rs, db2_ss, db2_rs, hid_ls,
+    dw2_ss, dw2_rs, db2_ss, db2_rs, turn_sem,
 ):
     xb, hb = act.at[0], act.at[1]
     s = lax.axis_index("s")
@@ -71,9 +72,10 @@
     far = [lax.rem(quad + k, QUADS) for k in (2, 1, 3)]
     near = [lax.rem(quad + QUADS - k, QUADS) for k in (2, 1, 3)]
     own_half = lax.rem(y, 2)
-    user_y = 2 * x + y // 2
-    owner_x = y // 2
-    owner_y = [2 * own_half + p for p in range(2)]
+    user_y = 2 * (y // 2) + x
+    owner_x = own_half
+    owner_y = [2 * (y // 2) + p for p in range(2)]
+    own_block = 2 * own_half + y // 2
 
     def is_me(zz, xx, yy):
         return (zz == z) & (xx == x) & (yy == y)
@@ -146,7 +148,7 @@
     st_own.start()
 
     def win_copy(gate, half):
-        first = pl.multiple_of(gate * D + half * Y * LANES + y * LANES, LANES)
+        first = pl.multiple_of(gate * D + half * Y * LANES + own_block * LANES, LANES)
         block = gate * 2 + half
         return pltpu.make_async_copy(
             win_hbm.at[:, pl.ds(first, LANES)],
@@ -193,7 +195,7 @@
         for t in range(STEPS):
             for half in range(2):
                 for yy in range(Y):
-                    first = (half * Y + yy) * LANES
+                    first = (half * Y + ORDER[yy]) * LANES
                     xb[t, half, yy, y] = obs_st[t, :, first : first + LANES]
         for k in range(Y - 1):
             obs_copy(k).start()
@@ -213,7 +215,7 @@
         for t in range(STEPS):
             for half in range(2):
                 for yy in range(Y):
-                    first = (half * Y + yy) * LANES
+                    first = (half * Y + ORDER[yy]) * LANES
                     cot_st[yy, t, half] = cot_in[t, :, first : first + LANES]
         for t in range(STEPS):
             for half in range(2):
@@ -246,6 +248,8 @@
                 if step < Z // 2 and ring_has(way, step, p):
                     ring(way, step, p).start()
 
+    leads = lax.rem(s, 2) == 0
+
     def turn_block(plane):
         block = wrt[plane].reshape(LANES, D)
         for n in range(2 * Y):
@@ -263,8 +267,10 @@
                 part, part, wa_ss.at[0], wa_rs.at[p], {"x": owner_x, "y": owner_y[p]}
             ).wait_recv()
 
-        for way in range(2):
-            ring(way, 0, p).start()
+        @pl.when(leads)
+        def _():
+            for way in range(2):
+                ring(way, 0, p).start()
 
     st_own.wait()
     for k in range(S - 1):
@@ -280,7 +286,7 @@
 
     for half in range(2):
         for yy in range(Y):
-            first = (half * Y + yy) * LANES
+            first = (half * Y + ORDER[yy]) * LANES
             hb[0, half, yy, y] = chosen(first)
             c_st[yy, half] = chosen(D + first)
     c_in[y] = c_st[y]
@@ -305,6 +311,14 @@
         c0_copy(k).start()
 
     turn_block(z)
+
+    @pl.when(jnp.logical_not(leads))
+    def _():
+        pl.semaphore_wait(turn_sem, 1)
+        for p in range(2):
+            for way in range(2):
+                ring(way, 0, p).start()
+
     ring_turn(1)
     turn_block(z_up)
     turn_block(z_down)
@@ -319,6 +333,11 @@
         cells[0, half] = c_in[:, half].reshape(ALL_ROWS, LANES).astype(F32)
 
     ring_turn(2)
+
+    @pl.when(leads)
+    def _():
+        pl.semaphore_signal(turn_sem, inc=1, device_id={"s": up_s[0]}, device_id_type=MESH)
+
     turn_block(lax.rem(z + 2, Z))
     turn_block(lax.rem(z + Z - 2, Z))
     for gate in range(GATES):
@@ -358,14 +377,13 @@
 
     ring_turn(4)
     turn_block(lax.rem(z + Z // 2, Z))
-    hz_copy(0).start()
 
     def whole(ref, *at):
         return jnp.concatenate(
             [
                 ref[(*at, half, yy)].reshape(ALL_ROWS, LANES)
                 for half in range(2)
-                for yy in range(Y)
+                for yy in ORDER
             ],
             axis=1,
         )
@@ -395,6 +413,10 @@
         @pl.when(t < STEPS - 1)
         def _():
             hz_copy(t + 1).start()
+
+        @pl.when(t == 0)
+        def _():
+            hz_copy(0).start()
 
     def product(kind, inputs, gate):
         weights = jnp.concatenate([wts[kind, 2 * gate], wts[kind, 2 * gate + 1]], axis=1)
@@ -405,7 +427,7 @@
         for gate in range(GATES):
             part = product(kind, inputs, gate)
             for half in range(2):
-                first = pl.multiple_of(gate * D + half * Y * LANES + y * LANES, LANES)
+                first = pl.multiple_of(gate * D + half * Y * LANES + own_block * LANES, LANES)
                 acc[gate, half] = (
                     part[:, half * LANES : (half + 1) * LANES] + bias_ref[:, pl.ds(first, LANES)]
                 )
@@ -444,15 +466,13 @@
             h_copy(t + 1, k).start()
 
     pass_up(STEPS - 1)
-    hid_copy = pltpu.make_async_copy(hid_st, hid_out, hid_ls)
 
     def keep_hidden():
         for t in range(STEPS):
             for half in range(2):
                 for yy in range(Y):
-                    first = (half * Y + yy) * LANES
-                    hid_st[t, :, first : first + LANES] = hb[t + 1, half, yy, y]
-        hid_copy.start()
+                    first = (half * Y + ORDER[yy]) * LANES
+                    hid_out[t, :, first : first + LANES] = hb[t + 1, half, yy, y]
         for t in range(STEPS):
             hz_arrival(t).wait_recv()
             hmat[t * ALL_ROWS : (t + 1) * ALL_ROWS, :] = whole(hb, t)
@@ -547,7 +567,7 @@
                 ).astype(BF16)
                 for n in range(2):
                     block = 2 * j + n
-                    a_send[t, block % Y, block // Y] = part[:, n * LANES : (n + 1) * LANES]
+                    a_send[t, ORDER[block % Y], block // Y] = part[:, n * LANES : (n + 1) * LANES]
             for k in range(Y - 1):
                 a_copy(t, k).start()
 
@@ -560,7 +580,7 @@
                 ).astype(BF16)
                 for n in range(2):
                     block = 2 * j + n
-                    g_send[t, block % Y, block // Y] = part[:, n * LANES : (n + 1) * LANES]
+                    g_send[t, ORDER[block % Y], block // Y] = part[:, n * LANES : (n + 1) * LANES]
             for k in range(Y - 1):
                 g_copy(t, k).start()
 
@@ -583,15 +603,15 @@
                 )
             e_copy(t).start()
 
-    def dw_copy(k):
-        return remote(
-            dw_send.at[far[k]], dw_recv.at[quad], dw_ss.at[k], dw_rs.at[k],
+    def dw_copy(k, p):
+        return remote(
+            dw_send.at[far[k], p], dw_recv.at[quad, p], dw_ss.at[k, p], dw_rs.at[k, p],
             {"z": 2 * far[k] + z_half},
         )
 
-    def dw_arrival(k):
-        part = dw_recv.at[near[k]]
-        return remote(part, part, dw_ss.at[k], dw_rs.at[k], {"z": 2 * far[k] + z_half})
+    def dw_arrival(k, p):
+        part = dw_recv.at[near[k], p]
+        return remote(part, part, dw_ss.at[k, p], dw_rs.at[k, p], {"z": 2 * far[k] + z_half})
 
     def db_copy(k):
         return remote(
@@ -628,12 +648,16 @@
             columns = slice(j * 2 * LANES, (j + 1) * 2 * LANES)
             part = dw_acc[gate, :, columns] + nn_dot(rows_pair, hmat_pair[:ALL_ROWS, columns])
             if k < QUADS - 1:
-                dw_send[gate, :, columns] = part.astype(BF16)
+                for p in range(2):
+                    rows = slice(p * LANES // 2, (p + 1) * LANES // 2)
+                    dw_send[gate, p, :, columns] = part[rows].astype(BF16)
             else:
                 dw_acc[gate, :, columns] = part
         if k < QUADS - 1:
             db_copy(k).start()
-            dw_copy(k).start()
+            dw_copy(k, 0).start()
+    for k in range(QUADS - 1):
+        dw_copy(k, 1).start()
 
     def dw2_copy(p):
         return remote(
@@ -650,13 +674,13 @@
     for k in range(QUADS - 1):
         db_arrival(k).wait_recv()
     db2_send[...] = db_send[quad] + db_recv[near[0]] + db_recv[near[1]] + db_recv[near[2]]
-    for k in range(QUADS - 1):
-        dw_arrival(k).wait_recv()
     for p in range(2):
         rows = slice(p * LANES // 2, (p + 1) * LANES // 2)
+        for k in range(QUADS - 1):
+            dw_arrival(k, p).wait_recv()
         value = dw_acc[quad, rows, :]
         for k in range(QUADS - 1):
-            value = value + dw_recv[near[k], rows, :].astype(F32)
+            value = value + dw_recv[near[k], p].astype(F32)
         dw2_send[p] = value.astype(BF16)
 
         @pl.when(is_me(z, owner_x, owner_y[p]))
@@ -733,15 +757,14 @@
             e_copy(t).wait_send()
 
     for k in range(QUADS - 1):
-        dw_copy(k).wait_send()
+        for p in range(2):
+            dw_copy(k, p).wait_send()
         db_copy(k).wait_send()
     for p in range(2):
         @pl.when(jnp.logical_not(is_me(z, owner_x, owner_y[p])))
         def _():
             dw2_copy(p).wait_send()
             db2_copy(p).wait_send()
-
-    hid_copy.wait()
 
 
 def on_device(
@@ -754,12 +777,12 @@
     hidden, weights, biases = pl.pallas_call(
         kernel,
         out_shape=(
-            jax.ShapeDtypeStruct((STEPS, ROWS, D), BF16),
-            jax.ShapeDtypeStruct((LANES // 2, D), F32),
-            jax.ShapeDtypeStruct((1, LANES // 2), F32),
+            pltpu.VMEM((STEPS, ROWS, D), BF16),
+            pltpu.VMEM((LANES // 2, D), F32),
+            pltpu.VMEM((1, LANES // 2), F32),
         ),
         in_specs=[hbm, hbm, hbm, hbm, vmem, hbm, vmem, vmem, vmem],
-        out_specs=(hbm, vmem, vmem),
+        out_specs=(vmem, vmem, vmem),
         scratch_shapes=[
             pltpu.VMEM((STEPS, ROWS, D), BF16),
             pltpu.VMEM((STEPS, ROWS, D), BF16),
@@ -790,15 +813,14 @@
             pltpu.VMEM((STEPS * ALL_ROWS, D), BF16),
             pltpu.VMEM((STEPS * ALL_ROWS, D), BF16),
             pltpu.VMEM((GATES, LANES, D), F32),
-            pltpu.VMEM((GATES, LANES, D), BF16),
-            pltpu.VMEM((GATES, LANES, D), BF16),
+            pltpu.VMEM((GATES, 2, LANES // 2, D), BF16),
+            pltpu.VMEM((GATES, 2, LANES // 2, D), BF16),
             pltpu.VMEM((GATES, 8, LANES), F32),
             pltpu.VMEM((GATES, 8, LANES), F32),
             pltpu.VMEM((2, LANES // 2, D), BF16),
             pltpu.VMEM((X, LANES // 2, D), BF16),
             pltpu.VMEM((8, LANES), F32),
             pltpu.VMEM((X, 8, LANES), F32),
-            pltpu.VMEM((STEPS, ROWS, D), BF16),
             dma((2,)),
             dma((Y - 1,)), dma((Y - 1,)),
             dma((S - 1,)), dma((S - 1,)), dma,
@@ -815,11 +837,11 @@
             dma((STEPS, Y - 1)), dma((STEPS, Y - 1)),
             dma((STEPS, Y - 1)), dma((STEPS, Y - 1)),
             dma((STEPS,)), dma((STEPS,)),
-            dma((3,)), dma((3,)),
+            dma((3, 2)), dma((3, 2)),
             dma((3,)), dma((3,)),
             dma((2,)), dma((X,)),
             dma((2,)), dma((X,)),
-            dma,
+            pltpu.SemaphoreType.REGULAR,
         ],
         compiler_params=pltpu.CompilerParams(
             collective_id=0, has_side_effects=True, vmem_limit_bytes=56 * 1024 * 1024

time: 180 us -> 173 us (0.961)
  Pallas kernels: 173 us -> 170 us
  local copies, waits for them, and re-layouts: 4.45 us -> 1.92 us
    pallas_call x1, Pallas kernels: 173 us -> 170 us  [on_device(): pl.pallas_call(kernel, out_shape=(pltpu.VMEM((STEPS, ROWS, D), BF16), plt...]
    unnamed x3, local copies, waits for them, and re-layouts: 4.45 us -> 1.92 us
where the time goes in v3:
time: 173 us; the launch traced here: 172 us
  Pallas kernels  170 us (98%)
  local copies, waits for them, and re-layouts  1.92 us (1%)
    pallas_call x1, Pallas kernels, on_device(): pl.pallas_call(kernel, out_shape=(pltpu.VMEM((STEPS, ROWS, D), BF16), plt...  170 us

profile of v3, /device:TPU:24, one launch (start us, length us, event | category | flops | bytes accessed | tf_op | source)
XLA Modules:
  0.0 172.3 jit_solution(11577556107055239853)
XLA Ops:
  0.6 169.7 %replay_window.1 = (bf16[4,32,1024]{2,1,0:T(8,128)(2,1)S(1)}, f32[64,1024]{1,0:T(8,128)S(1)}, f32[1,64]{1,0:T(1,128)S(1)}) custom-call(bf16[4,32,1024]{2,1,0:T(8,128)(2,1)} %obs_hbm.1, bf16[4,32,1024]{2,1,0:T(8,128)(2,1)} %cot_hbm.1, bf16[1024,4096]{1,0:T(8,128)(2,1)} %bitcast.14, bf16[64,1024]{1,0:T(8,128)(2,1)} %bitcast.16, f32[1,4096]{1,0:T(1,128)} %bias_ref.1, ...), custom_call_target="tpu_custom_call" | custom-call | tf_op jit(solution)/shard_map/replay_window/pallas_call | solution.py:777
  170.4 0.7 copy.15
  171.1 0.7 copy.16
  171.8 0.5 copy.17

commit v4 on v3

--- a/solution.py
+++ b/solution.py
@@ -14,6 +14,9 @@
 ORDER = (0, 2, 1, 3)
 GATES = 4
 ALL_ROWS = Y * ROWS
+PARTS = 2
+GROUPS = Y // PARTS
+PART_ROWS = ALL_ROWS // PARTS
 LOCAL = GATES * 2 * LANES
 MESH = pl.DeviceIdType.MESH
 BF16 = jnp.bfloat16
@@ -293,11 +296,11 @@
 
     def h0_copy(k):
         part = hb.at[0, :, :, y]
-        return remote(part, part, h_ss.at[0, k], h_rs.at[0, k], {"y": up_y[k]})
+        return remote(part, part, h_ss.at[0, 0, k], h_rs.at[0, 0, k], {"y": up_y[k]})
 
     def h0_arrival(k):
         part = hb.at[0, :, :, down_y[k]]
-        return remote(part, part, h_ss.at[0, k], h_rs.at[0, k], {"y": up_y[k]})
+        return remote(part, part, h_ss.at[0, 0, k], h_rs.at[0, 0, k], {"y": up_y[k]})
 
     def c0_copy(k):
         return remote(c_st.at[up_y[k]], c_in.at[y], c_ss.at[k], c_rs.at[k], {"y": up_y[k]})
@@ -328,9 +331,16 @@
     marks_all = info[...].reshape(ALL_ROWS, LANES)
     for t in range(STEPS):
         alive_now = (marks_all[:, 0:1] <= float(t)) & (marks_all[:, 1:2] > float(t))
-        live[t] = jnp.broadcast_to(jnp.where(alive_now, 1.0, 0.0), (ALL_ROWS, LANES))
+        live[t] = jnp.broadcast_to(jnp.where(alive_now, 1.0, 0.0), (ALL_ROWS, LANES)).reshape(
+            PARTS, PART_ROWS, LANES
+        )
     for half in range(2):
-        cells[0, half] = c_in[:, half].reshape(ALL_ROWS, LANES).astype(F32)
+        for part in range(PARTS):
+            cells[0, part, half] = (
+                c_in[part * GROUPS : (part + 1) * GROUPS, half]
+                .reshape(PART_ROWS, LANES)
+                .astype(F32)
+            )
 
     ring_turn(2)
 
@@ -388,33 +398,50 @@
             axis=1,
         )
 
-    def h_copy(t, k):
-        part = hb.at[t, :, y]
-        return remote(part, part, h_ss.at[t, k], h_rs.at[t, k], {"y": up_y[k]})
-
-    def h_arrival(t, k):
-        part = hb.at[t, :, down_y[k]]
-        return remote(part, part, h_ss.at[t, k], h_rs.at[t, k], {"y": up_y[k]})
-
-    def x_copy(t):
-        return remote(hb.at[t + 1], xb.at[t], x_ss.at[t], x_rs.at[t], {"s": up_s[0]})
-
-    def x_arrival(t):
-        return remote(xb.at[t], xb.at[t], x_ss.at[t], x_rs.at[t], {"s": up_s[0]})
-
-    def pass_up(t):
+    def groups(b):
+        return pl.ds(b * GROUPS, GROUPS)
+
+    def rows_of(kind, t, b):
+        return jnp.concatenate(
+            [
+                act[kind, t, half, yy, groups(b)].reshape(PART_ROWS, LANES)
+                for half in range(2)
+                for yy in ORDER
+            ],
+            axis=1,
+        )
+
+    def h_copy(t, b, k):
+        part = hb.at[t, :, y, groups(b)]
+        return remote(part, part, h_ss.at[t, b, k], h_rs.at[t, b, k], {"y": up_y[k]})
+
+    def h_arrival(t, b, k):
+        part = hb.at[t, :, down_y[k], groups(b)]
+        return remote(part, part, h_ss.at[t, b, k], h_rs.at[t, b, k], {"y": up_y[k]})
+
+    def x_copy(t, b):
+        return remote(
+            hb.at[t + 1, :, :, groups(b)], xb.at[t, :, :, groups(b)],
+            x_ss.at[t, b], x_rs.at[t, b], {"s": up_s[0]},
+        )
+
+    def x_arrival(t, b):
+        part = xb.at[t, :, :, groups(b)]
+        return remote(part, part, x_ss.at[t, b], x_rs.at[t, b], {"s": up_s[0]})
+
+    def pass_up(t, b):
         for k in range(Y - 1):
-            h_arrival(t + 1, k).wait_recv()
+            h_arrival(t + 1, b, k).wait_recv()
 
         @pl.when(s < S - 1)
         def _():
-            x_copy(t).start()
-
-        @pl.when(t < STEPS - 1)
+            x_copy(t, b).start()
+
+        @pl.when((t < STEPS - 1) & (b == PARTS - 1))
         def _():
             hz_copy(t + 1).start()
 
-        @pl.when(t == 0)
+        @pl.when((t == 0) & (b == PARTS - 1))
         def _():
             hz_copy(0).start()
 
@@ -422,50 +449,57 @@
         weights = jnp.concatenate([wts[kind, 2 * gate], wts[kind, 2 * gate + 1]], axis=1)
         return nn_dot(inputs, weights)
 
-    def first_product(kind, t):
-        inputs = whole(act, kind, t)
+    def first_product(kind, t, b):
+        inputs = rows_of(kind, t, b)
         for gate in range(GATES):
             part = product(kind, inputs, gate)
             for half in range(2):
-                first = pl.multiple_of(gate * D + half * Y * LANES + own_block * LANES, LANES)
+                first = pl.multiple_of(
+                    gate * D + half * Y * LANES + own_block * LANES, LANES
+                )
                 acc[gate, half] = (
                     part[:, half * LANES : (half + 1) * LANES] + bias_ref[:, pl.ds(first, LANES)]
                 )
 
     last_kind = jnp.where(s == 0, 1, 0)
 
-    @pl.loop(0, STEPS)
-    def _(t):
+    @pl.loop(0, STEPS * PARTS)
+    def _(turn):
+        t = turn // PARTS
+        b = lax.rem(turn, PARTS)
+
         @pl.when(s == 0)
         def _():
-            first_product(0, t)
+            first_product(0, t, b)
 
         @pl.when(t > 0)
         def _():
-            pass_up(t - 1)
+            pass_up(t - 1, b)
 
         @pl.when(s > 0)
         def _():
-            first_product(1, t)
-            x_arrival(t).wait_recv()
-
-        inputs = whole(act, last_kind, t)
+            first_product(1, t, b)
+            x_arrival(t, b).wait_recv()
+
+        inputs = rows_of(last_kind, t, b)
         for gate in range(GATES):
             part = product(last_kind, inputs, gate)
             for half in range(2):
                 pre = acc[gate, half] + part[:, half * LANES : (half + 1) * LANES]
-                gates[t, gate, half] = jnp.tanh(pre) if gate == 2 else sigmoid(pre)
+                gates[t, b, gate, half] = jnp.tanh(pre) if gate == 2 else sigmoid(pre)
         for half in range(2):
             cell = (
-                gates[t, 1, half] * cells[t, half] + gates[t, 0, half] * gates[t, 2, half]
+                gates[t, b, 1, half] * cells[t, b, half]
+                + gates[t, b, 0, half] * gates[t, b, 2, half]
             )
-            cells[t + 1, half] = cell
-            hidden = (gates[t, 3, half] * jnp.tanh(cell)).astype(BF16)
-            hb[t + 1, half, y] = hidden.reshape(Y, ROWS, LANES)
+            cells[t + 1, b, half] = cell
+            hidden = (gates[t, b, 3, half] * jnp.tanh(cell)).astype(BF16)
+            hb[t + 1, half, y, groups(b)] = hidden.reshape(GROUPS, ROWS, LANES)
         for k in range(Y - 1):
-            h_copy(t + 1, k).start()
-
-    pass_up(STEPS - 1)
+            h_copy(t + 1, b, k).start()
+
+    for part in range(PARTS):
+        pass_up(STEPS - 1, part)
 
     def keep_hidden():
         for t in range(STEPS):
@@ -489,119 +523,136 @@
         part = grads_pair.at[t]
         return remote(part, part, gz_ss.at[t], gz_rs.at[t], {"z": z_pair})
 
-    def a_copy(t, k):
-        return remote(
-            a_send.at[t, up_y[k]], a_recv.at[t, y], a_ss.at[t, k], a_rs.at[t, k], {"y": up_y[k]}
-        )
-
-    def a_arrival(t, k):
-        part = a_recv.at[t, down_y[k]]
-        return remote(part, part, a_ss.at[t, k], a_rs.at[t, k], {"y": up_y[k]})
-
-    def g_copy(t, k):
-        return remote(
-            g_send.at[t, up_y[k]], g_recv.at[t, y], g_ss.at[t, k], g_rs.at[t, k], {"y": up_y[k]}
-        )
-
-    def g_arrival(t, k):
-        part = g_recv.at[t, down_y[k]]
-        return remote(part, part, g_ss.at[t, k], g_rs.at[t, k], {"y": up_y[k]})
-
-    def e_copy(t):
-        return remote(e_send.at[t], eb.at[t], e_ss.at[t], e_rs.at[t], {"s": down_s[0]})
-
-    def e_arrival(t):
-        return remote(eb.at[t], eb.at[t], e_ss.at[t], e_rs.at[t], {"s": down_s[0]})
-
-    def total(sent, received, t, half):
-        value = sent[t, y, half].astype(F32)
+    def a_copy(t, b, k):
+        return remote(
+            a_send.at[t, b, up_y[k]], a_recv.at[t, b, y], a_ss.at[t, b, k], a_rs.at[t, b, k],
+            {"y": up_y[k]},
+        )
+
+    def a_arrival(t, b, k):
+        part = a_recv.at[t, b, down_y[k]]
+        return remote(part, part, a_ss.at[t, b, k], a_rs.at[t, b, k], {"y": up_y[k]})
+
+    def g_copy(t, b, k):
+        return remote(
+            g_send.at[t, b, up_y[k]], g_recv.at[t, b, y], g_ss.at[t, b, k], g_rs.at[t, b, k],
+            {"y": up_y[k]},
+        )
+
+    def g_arrival(t, b, k):
+        part = g_recv.at[t, b, down_y[k]]
+        return remote(part, part, g_ss.at[t, b, k], g_rs.at[t, b, k], {"y": up_y[k]})
+
+    def e_copy(t, b):
+        return remote(
+            e_send.at[t, b], eb.at[t, :, groups(b)], e_ss.at[t, b], e_rs.at[t, b],
+            {"s": down_s[0]},
+        )
+
+    def e_arrival(t, b):
+        part = eb.at[t, :, groups(b)]
+        return remote(part, part, e_ss.at[t, b], e_rs.at[t, b], {"s": down_s[0]})
+
+    def total(sent, received, t, b, half):
+        value = sent[t, b, y, half].astype(F32)
         for k in range(Y - 1):
-            value = value + received[t, down_y[k], half].astype(F32)
+            value = value + received[t, b, down_y[k], half].astype(F32)
         return value
 
-    @pl.loop(0, STEPS)
-    def _(back):
+    def hand_down(t, b):
+        for k in range(Y - 1):
+            g_arrival(t, b, k).wait_recv()
+        for half in range(2):
+            e_send[t, b, half] = (
+                total(g_send, g_recv, t, b, half).astype(BF16).reshape(GROUPS, ROWS, LANES)
+            )
+        e_copy(t, b).start()
+
+    def spread(sent, t, b, gate_grads, weights):
+        for j in range(4):
+            columns = slice(j * 2 * LANES, (j + 1) * 2 * LANES)
+            part = nn_dot(gate_grads, weights(columns)).astype(BF16)
+            for n in range(2):
+                block = 2 * j + n
+                sent[t, b, ORDER[block % Y], block // Y] = part[:, n * LANES : (n + 1) * LANES]
+
+    @pl.loop(0, STEPS * PARTS)
+    def _(turn):
+        back = turn // PARTS
+        b = lax.rem(turn, PARTS)
         t = STEPS - 1 - back
 
         @pl.when(s < S - 1)
         def _():
-            e_arrival(t).wait_recv()
+            e_arrival(t, b).wait_recv()
 
         for half in range(2):
-            acc[0, half] = eb[t, half].reshape(ALL_ROWS, LANES).astype(F32)
+            acc[0, half] = eb[t, half, groups(b)].reshape(PART_ROWS, LANES).astype(F32)
 
         @pl.when(back > 0)
         def _():
             for k in range(Y - 1):
-                a_arrival(t + 1, k).wait_recv()
+                a_arrival(t + 1, b, k).wait_recv()
             for half in range(2):
-                acc[0, half] = acc[0, half] + total(a_send, a_recv, t + 1, half)
+                acc[0, half] = acc[0, half] + total(a_send, a_recv, t + 1, b, half)
 
         for half in range(2):
-            in_gate = gates[t, 0, half]
-            forget = gates[t, 1, half]
-            candidate = gates[t, 2, half]
-            out_gate = gates[t, 3, half]
-            alive = live[t]
+            in_gate = gates[t, b, 0, half]
+            forget = gates[t, b, 1, half]
+            candidate = gates[t, b, 2, half]
+            out_gate = gates[t, b, 3, half]
+            alive = live[t, b]
             total_h = acc[0, half]
-            squashed = jnp.tanh(cells[t + 1, half])
-            total_c = carry[half] + total_h * out_gate * (1.0 - squashed * squashed)
+            squashed = jnp.tanh(cells[t + 1, b, half])
+            total_c = carry[b, half] + total_h * out_gate * (1.0 - squashed * squashed)
             parts = (
                 total_c * candidate * in_gate * (1.0 - in_gate) * alive,
-                total_c * cells[t, half] * forget * (1.0 - forget) * alive,
+                total_c * cells[t, b, half] * forget * (1.0 - forget) * alive,
                 total_c * in_gate * (1.0 - candidate * candidate) * alive,
                 total_h * squashed * out_gate * (1.0 - out_gate) * alive,
             )
-            carry[half] = total_c * forget * alive
+            carry[b, half] = total_c * forget * alive
             for gate in range(GATES):
-                grads[2 * gate + half] = parts[gate].astype(BF16)
-
-        gate_grads = jnp.concatenate([grads[block] for block in range(2 * GATES)], axis=1)
+                grads[b, 2 * gate + half] = parts[gate].astype(BF16)
+
+        gate_grads = jnp.concatenate([grads[b, block] for block in range(2 * GATES)], axis=1)
 
         @pl.when(t > 0)
         def _():
-            for j in range(4):
-                columns = slice(j * 2 * LANES, (j + 1) * 2 * LANES)
-                part = nn_dot(
-                    gate_grads, wrt[:, :, :, columns].reshape(LOCAL, 2 * LANES)
-                ).astype(BF16)
-                for n in range(2):
-                    block = 2 * j + n
-                    a_send[t, ORDER[block % Y], block // Y] = part[:, n * LANES : (n + 1) * LANES]
+            spread(
+                a_send, t, b, gate_grads,
+                lambda columns: wrt[:, :, :, columns].reshape(LOCAL, 2 * LANES),
+            )
             for k in range(Y - 1):
-                a_copy(t, k).start()
+                a_copy(t, b, k).start()
 
         @pl.when(s > 0)
         def _():
-            for j in range(4):
-                columns = slice(j * 2 * LANES, (j + 1) * 2 * LANES)
-                part = nn_dot(
-                    gate_grads, wint[:, :, columns].reshape(LOCAL, 2 * LANES)
-                ).astype(BF16)
-                for n in range(2):
-                    block = 2 * j + n
-                    g_send[t, ORDER[block % Y], block // Y] = part[:, n * LANES : (n + 1) * LANES]
+            spread(
+                g_send, t, b, gate_grads,
+                lambda columns: wint[:, :, columns].reshape(LOCAL, 2 * LANES),
+            )
             for k in range(Y - 1):
-                g_copy(t, k).start()
-
-        for gate in range(GATES):
-            for half in range(2):
-                grads_t[t, half, gate] = grads[2 * gate + half].T
-        gz_copy(t).start()
-
-        @pl.when(back == 0)
-        def _():
-            keep_hidden()
-
-        @pl.when(s > 0)
-        def _():
-            for k in range(Y - 1):
-                g_arrival(t, k).wait_recv()
-            for half in range(2):
-                e_send[t, half] = total(g_send, g_recv, t, half).astype(BF16).reshape(
-                    Y, ROWS, LANES
-                )
-            e_copy(t).start()
+                g_copy(t, b, k).start()
+
+        @pl.when(b == PARTS - 1)
+        def _():
+            for gate in range(GATES):
+                for half in range(2):
+                    block = jnp.concatenate(
+                        [grads[part, 2 * gate + half] for part in range(PARTS)], axis=0
+                    )
+                    grads_t[t, half, gate] = block.T
+            gz_copy(t).start()
+
+            @pl.when(s > 0)
+            def _():
+                for part in range(PARTS):
+                    hand_down(t, part)
+
+            @pl.when(back == 0)
+            def _():
+                keep_hidden()
 
     def dw_copy(k, p):
         return remote(
@@ -735,26 +786,26 @@
 
     @pl.loop(0, STEPS)
     def _(t):
-        for k in range(Y - 1):
-            h_copy(t + 1, k).wait_send()
-
-        @pl.when(s < S - 1)
-        def _():
-            x_copy(t).wait_send()
-
         hz_copy(t).wait_send()
         gz_copy(t).wait_send()
-
-        @pl.when(t > 0)
-        def _():
+        for b in range(PARTS):
             for k in range(Y - 1):
-                a_copy(t, k).wait_send()
-
-        @pl.when(s > 0)
-        def _():
-            for k in range(Y - 1):
-                g_copy(t, k).wait_send()
-            e_copy(t).wait_send()
+                h_copy(t + 1, b, k).wait_send()
+
+            @pl.when(s < S - 1)
+            def _():
+                x_copy(t, b).wait_send()
+
+            @pl.when(t > 0)
+            def _():
+                for k in range(Y - 1):
+                    a_copy(t, b, k).wait_send()
+
+            @pl.when(s > 0)
+            def _():
+                for k in range(Y - 1):
+                    g_copy(t, b, k).wait_send()
+                e_copy(t, b).wait_send()
 
     for k in range(QUADS - 1):
         for p in range(2):
@@ -797,19 +848,19 @@
             pltpu.VMEM((Y, STEPS, 2, ROWS, LANES), BF16),
             pltpu.VMEM((Y, 2, ROWS, LANES), BF16),
             pltpu.VMEM((Y, 2, ROWS, LANES), BF16),
-            pltpu.VMEM((STEPS + 1, 2, ALL_ROWS, LANES), F32),
-            pltpu.VMEM((STEPS, GATES, 2, ALL_ROWS, LANES), F32),
-            pltpu.VMEM((GATES, 2, ALL_ROWS, LANES), F32),
-            pltpu.VMEM((STEPS, ALL_ROWS, LANES), F32),
-            pltpu.VMEM((2 * GATES, ALL_ROWS, LANES), BF16),
+            pltpu.VMEM((STEPS + 1, PARTS, 2, PART_ROWS, LANES), F32),
+            pltpu.VMEM((STEPS, PARTS, GATES, 2, PART_ROWS, LANES), F32),
+            pltpu.VMEM((GATES, 2, PART_ROWS, LANES), F32),
+            pltpu.VMEM((STEPS, PARTS, PART_ROWS, LANES), F32),
+            pltpu.VMEM((PARTS, 2 * GATES, PART_ROWS, LANES), BF16),
             pltpu.VMEM((STEPS, 2, GATES, LANES, ALL_ROWS), BF16),
             pltpu.VMEM((STEPS, GATES, LANES, ALL_ROWS), BF16),
-            pltpu.VMEM((2, ALL_ROWS, LANES), F32),
-            pltpu.VMEM((STEPS, Y, 2, ALL_ROWS, LANES), BF16),
-            pltpu.VMEM((STEPS, Y, 2, ALL_ROWS, LANES), BF16),
-            pltpu.VMEM((STEPS, Y, 2, ALL_ROWS, LANES), BF16),
-            pltpu.VMEM((STEPS, Y, 2, ALL_ROWS, LANES), BF16),
-            pltpu.VMEM((STEPS, 2, *piece), BF16),
+            pltpu.VMEM((PARTS, 2, PART_ROWS, LANES), F32),
+            pltpu.VMEM((STEPS, PARTS, Y, 2, PART_ROWS, LANES), BF16),
+            pltpu.VMEM((STEPS, PARTS, Y, 2, PART_ROWS, LANES), BF16),
+            pltpu.VMEM((STEPS, PARTS, Y, 2, PART_ROWS, LANES), BF16),
+            pltpu.VMEM((STEPS, PARTS, Y, 2, PART_ROWS, LANES), BF16),
+            pltpu.VMEM((STEPS, PARTS, 2, GROUPS, ROWS, LANES), BF16),
             pltpu.VMEM((STEPS * ALL_ROWS, D), BF16),
             pltpu.VMEM((STEPS * ALL_ROWS, D), BF16),
             pltpu.VMEM((GATES, LANES, D), F32),
@@ -830,13 +881,13 @@
             dma((Y - 1,)), dma((Y - 1,)),
             dma((Y - 1,)), dma((Y - 1,)),
             dma((Y - 1,)), dma((Y - 1,)),
-            dma((STEPS + 1, Y - 1)), dma((STEPS + 1, Y - 1)),
+            dma((STEPS + 1, PARTS, Y - 1)), dma((STEPS + 1, PARTS, Y - 1)),
+            dma((STEPS, PARTS)), dma((STEPS, PARTS)),
             dma((STEPS,)), dma((STEPS,)),
             dma((STEPS,)), dma((STEPS,)),
-            dma((STEPS,)), dma((STEPS,)),
-            dma((STEPS, Y - 1)), dma((STEPS, Y - 1)),
-            dma((STEPS, Y - 1)), dma((STEPS, Y - 1)),
-            dma((STEPS,)), dma((STEPS,)),
+            dma((STEPS, PARTS, Y - 1)), dma((STEPS, PARTS, Y - 1)),
+            dma((STEPS, PARTS, Y - 1)), dma((STEPS, PARTS, Y - 1)),
+            dma((STEPS, PARTS)), dma((STEPS, PARTS)),
             dma((3, 2)), dma((3, 2)),
             dma((3,)), dma((3,)),
             dma((2,)), dma((X,)),

time: 173 us -> 166 us (0.960)
  Pallas kernels: 170 us -> 163 us
    pallas_call x1, Pallas kernels: 170 us -> 163 us  [on_device(): pl.pallas_call(kernel, out_shape=(pltpu.VMEM((STEPS, ROWS, D), BF16), plt...]
where the time goes in v4:
time: 166 us
  Pallas kernels  163 us (98%)
  local copies, waits for them, and re-layouts  1.92 us (1%)
    pallas_call x1, Pallas kernels, on_device(): pl.pallas_call(kernel, out_shape=(pltpu.VMEM((STEPS, ROWS, D), BF16), plt...  163 us

profile of v4, /device:TPU:24, one launch (start us, length us, event | category | flops | bytes accessed | tf_op | source)
XLA Modules:
  0.0 166.0 jit_solution(3006512225089851815)
XLA Ops:
  0.6 163.5 %replay_window.1 = (bf16[4,32,1024]{2,1,0:T(8,128)(2,1)S(1)}, f32[64,1024]{1,0:T(8,128)S(1)}, f32[1,64]{1,0:T(1,128)S(1)}) custom-call(bf16[4,32,1024]{2,1,0:T(8,128)(2,1)} %obs_hbm.1, bf16[4,32,1024]{2,1,0:T(8,128)(2,1)} %cot_hbm.1, bf16[1024,4096]{1,0:T(8,128)(2,1)} %bitcast.14, bf16[64,1024]{1,0:T(8,128)(2,1)} %bitcast.16, f32[1,4096]{1,0:T(1,128)} %bias_ref.1, ...), custom_call_target="tpu_custom_call" | custom-call | tf_op jit(solution)/shard_map/replay_window/pallas_call | solution.py:828
  164.1 0.7 copy.15
  164.8 0.7 copy.16
  165.5 0.5 copy.17

commit v5 on v4

--- a/solution.py
+++ b/solution.py
@@ -14,7 +14,7 @@
 ORDER = (0, 2, 1, 3)
 GATES = 4
 ALL_ROWS = Y * ROWS
-PARTS = 2
+PARTS = 4
 GROUPS = Y // PARTS
 PART_ROWS = ALL_ROWS // PARTS
 LOCAL = GATES * 2 * LANES

time: 166 us -> 165 us (level)
  Pallas kernels: 163 us -> 161 us
    pallas_call x1, Pallas kernels: 163 us -> 161 us  [on_device(): pl.pallas_call(kernel, out_shape=(pltpu.VMEM((STEPS, ROWS, D), BF16), plt...]
where the time goes in v5:
time: 165 us; the launch traced here: 164 us
  Pallas kernels  161 us (98%)
  local copies, waits for them, and re-layouts  1.92 us (1%)
    pallas_call x1, Pallas kernels, on_device(): pl.pallas_call(kernel, out_shape=(pltpu.VMEM((STEPS, ROWS, D), BF16), plt...  161 us

profile of v5, /device:TPU:24, one launch (start us, length us, event | category | flops | bytes accessed | tf_op | source)
XLA Modules:
  0.0 163.8 jit_solution(12860208708579931563)
XLA Ops:
  0.6 161.2 %replay_window.1 = (bf16[4,32,1024]{2,1,0:T(8,128)(2,1)S(1)}, f32[64,1024]{1,0:T(8,128)S(1)}, f32[1,64]{1,0:T(1,128)S(1)}) custom-call(bf16[4,32,1024]{2,1,0:T(8,128)(2,1)} %obs_hbm.1, bf16[4,32,1024]{2,1,0:T(8,128)(2,1)} %cot_hbm.1, bf16[1024,4096]{1,0:T(8,128)(2,1)} %bitcast.14, bf16[64,1024]{1,0:T(8,128)(2,1)} %bitcast.16, f32[1,4096]{1,0:T(1,128)} %bias_ref.1, ...), custom_call_target="tpu_custom_call" | custom-call | tf_op jit(solution)/shard_map/replay_window/pallas_call | solution.py:828
  161.8 0.7 copy.15
  162.5 0.7 copy.16
  163.2 0.5 copy.17

commit v6 on v5

--- a/solution.py
+++ b/solution.py
@@ -51,7 +51,7 @@
     hid_out, dw_out, db_out,
     obs_st, cot_in, info, st, wts, wrt, wint, act, hb_pair, eb, cot_st, c_st, c_in, cells, gates, acc, live,
     grads, grads_t, grads_pair, carry, a_send, a_recv, g_send, g_recv, e_send, hmat, hmat_pair,
-    dw_acc, dw_send, dw_recv, db_send, db_recv, dw2_send, dw2_recv, db2_send, db2_recv,
+    dw_acc, dw_send, dw_relay, dw_joint, dw_recv, db_send, db_recv, dw2_send, dw2_recv, db2_send, db2_recv,
     in_ls, info_ss, info_rs, st_ss, st_rs, st_ls, wa_ss, wa_rs, wa_ls, ring_ss, ring_rs, win_ls,
     obs_ss, obs_rs, cot_ss, cot_rs, c_ss, c_rs, h_ss, h_rs, x_ss, x_rs, hz_ss, hz_rs, gz_ss, gz_rs,
     a_ss, a_rs, g_ss, g_rs, e_ss, e_rs, dw_ss, dw_rs, db_ss, db_rs,
@@ -654,15 +654,31 @@
             def _():
                 keep_hidden()
 
-    def dw_copy(k, p):
-        return remote(
-            dw_send.at[far[k], p], dw_recv.at[quad, p], dw_ss.at[k, p], dw_rs.at[k, p],
-            {"z": 2 * far[k] + z_half},
-        )
-
-    def dw_arrival(k, p):
-        part = dw_recv.at[near[k], p]
-        return remote(part, part, dw_ss.at[k, p], dw_rs.at[k, p], {"z": 2 * far[k] + z_half})
+    up_quad, down_quad = far[1], far[2]
+    onward = [up_quad, down_quad]
+
+    def relay_copy(p):
+        return remote(
+            dw_send.at[far[0], p], dw_relay.at[p], dw_ss.at[0, p], dw_rs.at[0, p],
+            {"z": 2 * onward[p] + z_half},
+        )
+
+    def direct_copy(p):
+        return remote(
+            dw_send.at[onward[1 - p], p], dw_recv.at[0, p], dw_ss.at[1, p], dw_rs.at[1, p],
+            {"z": 2 * onward[1 - p] + z_half},
+        )
+
+    def joint_copy(p):
+        return remote(
+            dw_joint.at[p], dw_recv.at[1, p], dw_ss.at[2, p], dw_rs.at[2, p],
+            {"z": 2 * onward[p] + z_half},
+        )
+
+    def dw_wait(part, kind, p):
+        remote(
+            part, part, dw_ss.at[kind, p], dw_rs.at[kind, p], {"z": 2 * onward[p] + z_half}
+        ).wait_recv()
 
     def db_copy(k):
         return remote(
@@ -706,9 +722,11 @@
                 dw_acc[gate, :, columns] = part
         if k < QUADS - 1:
             db_copy(k).start()
-            dw_copy(k, 0).start()
-    for k in range(QUADS - 1):
-        dw_copy(k, 1).start()
+            if k == 0:
+                for p in range(2):
+                    relay_copy(p).start()
+            else:
+                direct_copy(2 - k).start()
 
     def dw2_copy(p):
         return remote(
@@ -722,16 +740,22 @@
             {"x": owner_x, "y": owner_y[p]},
         )
 
+    for p in range(2):
+        dw_wait(dw_relay.at[p], 0, p)
+        dw_joint[p] = (
+            dw_send[onward[p], p].astype(F32) + dw_relay[p].astype(F32)
+        ).astype(BF16)
+        joint_copy(p).start()
     for k in range(QUADS - 1):
         db_arrival(k).wait_recv()
     db2_send[...] = db_send[quad] + db_recv[near[0]] + db_recv[near[1]] + db_recv[near[2]]
     for p in range(2):
         rows = slice(p * LANES // 2, (p + 1) * LANES // 2)
-        for k in range(QUADS - 1):
-            dw_arrival(k, p).wait_recv()
+        for kind in range(2):
+            dw_wait(dw_recv.at[kind, p], kind + 1, p)
         value = dw_acc[quad, rows, :]
-        for k in range(QUADS - 1):
-            value = value + dw_recv[near[k], p].astype(F32)
+        for kind in range(2):
+            value = value + dw_recv[kind, p].astype(F32)
         dw2_send[p] = value.astype(BF16)
 
         @pl.when(is_me(z, owner_x, owner_y[p]))
@@ -808,9 +832,11 @@
                 e_copy(t, b).wait_send()
 
     for k in range(QUADS - 1):
-        for p in range(2):
-            dw_copy(k, p).wait_send()
         db_copy(k).wait_send()
+    for p in range(2):
+        relay_copy(p).wait_send()
+        direct_copy(p).wait_send()
+        joint_copy(p).wait_send()
     for p in range(2):
         @pl.when(jnp.logical_not(is_me(z, owner_x, owner_y[p])))
         def _():
@@ -865,7 +891,9 @@
             pltpu.VMEM((STEPS * ALL_ROWS, D), BF16),
             pltpu.VMEM((GATES, LANES, D), F32),
             pltpu.VMEM((GATES, 2, LANES // 2, D), BF16),
-            pltpu.VMEM((GATES, 2, LANES // 2, D), BF16),
+            pltpu.VMEM((2, LANES // 2, D), BF16),
+            pltpu.VMEM((2, LANES // 2, D), BF16),
+            pltpu.VMEM((2, 2, LANES // 2, D), BF16),
             pltpu.VMEM((GATES, 8, LANES), F32),
             pltpu.VMEM((GATES, 8, LANES), F32),
             pltpu.VMEM((2, LANES // 2, D), BF16),

time: 165 us -> 160 us (0.970)
  Pallas kernels: 161 us -> 157 us
    pallas_call x1, Pallas kernels: 161 us -> 157 us  [on_device(): pl.pallas_call(kernel, out_shape=(pltpu.VMEM((STEPS, ROWS, D), BF16), plt...]
where the time goes in v6:
time: 160 us
  Pallas kernels  157 us (98%)
  local copies, waits for them, and re-layouts  1.92 us (1%)
    pallas_call x1, Pallas kernels, on_device(): pl.pallas_call(kernel, out_shape=(pltpu.VMEM((STEPS, ROWS, D), BF16), plt...  157 us

profile of v6, /device:TPU:24, one launch (start us, length us, event | category | flops | bytes accessed | tf_op | source)
XLA Modules:
  0.0 159.6 jit_solution(14059375118871652691)
XLA Ops:
  0.6 157.0 %replay_window.1 = (bf16[4,32,1024]{2,1,0:T(8,128)(2,1)S(1)}, f32[64,1024]{1,0:T(8,128)S(1)}, f32[1,64]{1,0:T(1,128)S(1)}) custom-call(bf16[4,32,1024]{2,1,0:T(8,128)(2,1)} %obs_hbm.1, bf16[4,32,1024]{2,1,0:T(8,128)(2,1)} %cot_hbm.1, bf16[1024,4096]{1,0:T(8,128)(2,1)} %bitcast.14, bf16[64,1024]{1,0:T(8,128)(2,1)} %bitcast.16, f32[1,4096]{1,0:T(1,128)} %bias_ref.1, ...), custom_call_target="tpu_custom_call" | custom-call | tf_op jit(solution)/shard_map/replay_window/pallas_call | solution.py:854
  157.7 0.7 copy.15
  158.4 0.7 copy.16
  159.1 0.5 copy.17
